TPU v7x, 32 devices: a whole 2x2x4 slice. The times are simulated.
32 devices in a mesh: tok: 8 (over y, x, core), head: 4 (over z).
Axes of the slice: x: 2, y: 2, z: 4, core: 2. Of those that a mesh axis runs over, the one named last changes fastest.
Arguments:
- pre_tokens: bfloat16 [8192, 2048], P('tok'), may hold values from -6 to 6
- dec_tokens: bfloat16 [16, 2048], P('tok'), may hold values from -6 to 6
- attn_gain: float32 [2048], replicated, may hold values from 0.1 to 1.9
- mlp_gain: float32 [2048], replicated, may hold values from 0.1 to 1.9
- w_qkv: bfloat16 [3, 2048, 2048], P(None, 'head', 'tok'), may hold values from -0.125 to 0.125
- w_out: bfloat16 [2048, 2048], P('tok', 'head'), may hold values from -0.125 to 0.125
- w_gate_up: bfloat16 [2, 8192, 2048], P(None, 'head', 'tok'), may hold values from -0.125 to 0.125
- w_down: bfloat16 [2048, 8192], P('tok', 'head'), may hold values from -0.0625 to 0.0625
- pre_cache: bfloat16 [8, 2, 2048, 2048], P('tok', None, None, 'head'), may hold values from -60 to 60
- dec_cache: bfloat16 [16, 2, 4096, 2048], P('tok', None, None, 'head'), may hold values from -60 to 60
- pre_order: int32 [8], replicated, may hold values from 0 to 7, each once
- dec_order: int32 [16], replicated, may hold values from 0 to 15, each once
- pre_offsets: int32 [8], P('tok'), may hold values from 2 to 2048, as said below
- dec_lengths: int32 [16], P('tok'), may hold values from 2 to 4096, as said below
Outputs:
- pre_out: bfloat16 [8192, 2048], P('tok')
- dec_out: bfloat16 [16, 2048], P('tok')
Inputs may be any that keep to these rules, and one draw needn't show every extreme that they name: `pre_order`: the prefill request at position k is handled with the caches of position k, which lie on index k of tok. `dec_order`: positions k of one index of tok are those with k // 2 equal to it. `pre_offsets`: some position reaches 2048. `dec_lengths`: some position reaches 4096.
All inputs are finite; a program needn't handle non-finite values.
Results may differ from a plain program's by a relative error of at most 0.013.
Values may be sent and summed in bfloat16 or wider, within the bound.
A program may use at most 192 MiB of HBM per device.

v0:
```python
import jax
import jax.numpy as jnp
from jax import lax
from jax.sharding import PartitionSpec as P

HD = 64
BLOCK = 512


rope_base = 130000.0
norm_eps = 1e-05
masked_score = -1e30


def rotate(values, positions):
    width = values.shape[-1]
    half = width // 2
    freqs = rope_base ** (-(jnp.arange(half, dtype=jnp.float32) * 2.0 / width))
    angles = positions.astype(jnp.float32)[:, None] * freqs[None, :]
    cosine = jnp.cos(angles)[:, None, :]
    sine = jnp.sin(angles)[:, None, :]
    first = values[..., :half]
    second = values[..., half:]
    return jnp.concatenate(
        [first * cosine - second * sine, second * cosine + first * sine], axis=-1
    )


def rms_norm(rows, gain):
    rows = rows.astype(jnp.float32)
    factor = lax.rsqrt(jnp.mean(rows * rows, axis=-1, keepdims=True) + norm_eps)
    return (rows * factor * gain).astype(jnp.bfloat16)


def fold_rows(inputs, weights):
    return jnp.einsum(
        "td,kcd->ktc",
        inputs,
        lax.all_gather(weights, "tok", axis=2, tiled=True),
        preferred_element_type=jnp.float32,
    )


def map_rows(inputs, weights):
    return jnp.einsum(
        "tc,dc->td",
        inputs,
        lax.all_gather(weights, "tok", axis=0, tiled=True),
        preferred_element_type=jnp.float32,
    )


def over_heads(partial_value):
    return lax.psum(partial_value.astype(jnp.bfloat16), "head").astype(jnp.float32)


def attend_local(query, keys_new, values_new, positions, self_mask, cache, limit):
    rows_q = query.shape[0]
    heads = query.shape[1] // HD
    scale = 1.0 / jnp.sqrt(jnp.float32(HD))
    q_rot = rotate(query.reshape(rows_q, heads, HD).astype(jnp.float32), positions).astype(
        jnp.bfloat16
    )
    k_rot = rotate(keys_new.reshape(rows_q, heads, HD).astype(jnp.float32), positions).astype(
        jnp.bfloat16
    )
    v_new = values_new.reshape(rows_q, heads, HD)
    scores = jnp.einsum("qhd,khd->hqk", q_rot, k_rot, preferred_element_type=jnp.float32) * scale
    scores = jnp.where(self_mask[None], scores, masked_score)
    top = jnp.max(scores, axis=-1)
    weights = jnp.exp(scores - top[..., None])
    total = jnp.sum(weights, axis=-1)
    mixed = jnp.einsum(
        "hqk,khd->hqd", weights.astype(jnp.bfloat16), v_new, preferred_element_type=jnp.float32
    )
    cached = cache.reshape(2, cache.shape[1], heads, HD)

    def one_block(index, state):
        top_now, total_now, mixed_now = state
        begin = index * BLOCK
        keys_block = lax.dynamic_slice_in_dim(cached[0], begin, BLOCK, 0)
        values_block = lax.dynamic_slice_in_dim(cached[1], begin, BLOCK, 0)
        block_scores = (
            jnp.einsum("qhd,khd->hqk", q_rot, keys_block, preferred_element_type=jnp.float32)
            * scale
        )
        live = begin + jnp.arange(BLOCK, dtype=jnp.int32) < limit
        block_scores = jnp.where(live[None, None, :], block_scores, masked_score)
        new_top = jnp.maximum(top_now, jnp.max(block_scores, axis=-1))
        factor = jnp.exp(top_now - new_top)
        block_weights = jnp.exp(block_scores - new_top[..., None])
        total_next = total_now * factor + jnp.sum(block_weights, axis=-1)
        mixed_next = mixed_now * factor[..., None] + jnp.einsum(
            "hqk,khd->hqd",
            block_weights.astype(jnp.bfloat16),
            values_block,
            preferred_element_type=jnp.float32,
        )
        return (new_top, total_next, mixed_next)

    block_count = cache.shape[1] // BLOCK
    top, total, mixed = lax.fori_loop(0, block_count, one_block, (top, total, mixed))
    result = mixed / total[..., None]
    return jnp.transpose(result, (1, 0, 2)).reshape(rows_q, heads * HD).astype(jnp.bfloat16)


def on_device(
    pre_tokens,
    dec_tokens,
    attn_gain,
    mlp_gain,
    w_qkv,
    w_out,
    w_gate_up,
    w_down,
    pre_cache,
    dec_cache,
    pre_order,
    dec_order,
    pre_offsets,
    dec_lengths,
):
    tok_count = lax.axis_size("tok")
    tok_index = lax.axis_index("tok")
    span_rows = pre_tokens.shape[0]
    piece_len = span_rows // tok_count
    dec_local = dec_tokens.shape[0]
    dec_total = dec_order.shape[0]
    group_width = w_qkv.shape[1]
    rows = jnp.concatenate([pre_tokens, dec_tokens], axis=0)
    normed = rms_norm(rows, attn_gain)
    projected = fold_rows(normed, w_qkv).astype(jnp.bfloat16)
    pre_part = projected[:, :span_rows].reshape(3, tok_count, piece_len, group_width)
    pre_send = jnp.take(pre_part, pre_order, axis=1)
    dec_part = projected[:, span_rows:]
    dec_send = jnp.broadcast_to(dec_part[:, None], (3, tok_count, dec_local, group_width))
    pre_recv, dec_recv = (
        lax.all_to_all(pre_send, "tok", split_axis=1, concat_axis=1, tiled=True),
        lax.all_to_all(dec_send, "tok", split_axis=1, concat_axis=1, tiled=True),
    )
    pre_recv = pre_recv.reshape(3, span_rows, group_width)
    dec_recv = dec_recv.reshape(3, dec_total, group_width)
    offset_now = pre_offsets[0]
    pre_positions = offset_now + jnp.arange(span_rows, dtype=jnp.int32)
    causal = (
        jnp.arange(span_rows, dtype=jnp.int32)[None, :]
        <= jnp.arange(span_rows, dtype=jnp.int32)[:, None]
    )
    pre_att = attend_local(
        pre_recv[0], pre_recv[1], pre_recv[2], pre_positions, causal, pre_cache[0], offset_now
    )
    own_slots = lax.dynamic_slice_in_dim(dec_order, tok_index * dec_local, dec_local)
    dec_mine = jnp.take(dec_recv, own_slots, axis=1)
    self_only = jnp.ones((1, 1), jnp.bool_)
    dec_results = []
    for request in range(dec_local):
        length_now = dec_lengths[request]
        dec_results.append(
            attend_local(
                dec_mine[0, request : request + 1],
                dec_mine[1, request : request + 1],
                dec_mine[2, request : request + 1],
                dec_lengths[request : request + 1],
                self_only,
                dec_cache[request],
                length_now,
            )
        )
    dec_att = jnp.concatenate(dec_results, axis=0)
    picker = (jnp.arange(dec_total, dtype=jnp.int32)[:, None] == own_slots[None, :]).astype(
        jnp.bfloat16
    )
    dec_back = (
        jnp.dot(picker, dec_att, preferred_element_type=jnp.float32)
        .astype(jnp.bfloat16)
        .reshape(tok_count, dec_local, group_width)
    )
    pre_back = pre_att.reshape(tok_count, piece_len, group_width)
    pre_ret, dec_ret = (
        lax.all_to_all(pre_back, "tok", split_axis=0, concat_axis=0, tiled=True),
        lax.all_to_all(dec_back, "tok", split_axis=0, concat_axis=0, tiled=True),
    )
    slot_range = jnp.arange(tok_count, dtype=jnp.int32)
    inverse = jnp.sum(
        jnp.where(pre_order[None, :] == slot_range[:, None], slot_range[None, :], 0), axis=1
    )
    pre_mixed = jnp.take(pre_ret, inverse, axis=0).reshape(span_rows, group_width)
    dec_mixed = jnp.sum(dec_ret.astype(jnp.float32), axis=0).astype(jnp.bfloat16)
    attended = jnp.concatenate([pre_mixed, dec_mixed], axis=0)
    resid = rows.astype(jnp.float32) + over_heads(map_rows(attended, w_out))
    mlp_in = rms_norm(resid, mlp_gain)
    gate_up = fold_rows(mlp_in, w_gate_up)
    hidden = (jax.nn.silu(gate_up[0]) * gate_up[1]).astype(jnp.bfloat16)
    final = (resid + over_heads(map_rows(hidden, w_down))).astype(jnp.bfloat16)
    return (final[:span_rows], final[span_rows:])


def solution(mesh):
    placed = (
        P("tok", None),
        P("tok", None),
        P(),
        P(),
        P(None, "head", "tok"),
        P("tok", "head"),
        P(None, "head", "tok"),
        P("tok", "head"),
        P("tok", None, None, "head"),
        P("tok", None, None, "head"),
        P(),
        P(),
        P("tok"),
        P("tok"),
    )
    return jax.shard_map(
        on_device,
        mesh=mesh,
        in_specs=placed,
        out_specs=(P("tok", None), P("tok", None)),
        check_vma=False,
    )
```

profile of v0, /device:TPU:0, one launch (start us, length us, event | category | flops | bytes accessed | tf_op | source)
XLA Modules:
  0.0 917.4 jit_solution(6938060684797594388)
XLA Ops:
  22.7 11.3 %fusion.97 = (bf16[1,2,4096,512]{3,2,1,0:T(8,128)(2,1)}, bf16[1,2,4096,512]{3,2,1,0:T(8,128)(2,1)}) fusion(bf16[2,2,4096,512]{3,2,1,0:T(8,128)(2,1)} %param.29), kind=kLoop, calls=%fused_computation.196 | loop fusion | bytes 33554432 | tf_op jit(solution)/shard_map/slice | solution.py:165
  34.1 11.3 %copy.94 = bf16[1,2,4096,512]{2,3,1,0:T(8,128)(2,1)} copy(bf16[1,2,4096,512]{3,2,1,0:T(8,128)(2,1)} %get-tuple-element.511) | data formatting | bytes 16777216
  45.4 18.9 %copy.67 = bf16[2,4096,8,64]{3,2,1,0:T(8,128)(2,1)} copy(bf16[2,4096,8,64]{1,3,2,0:T(8,128)(2,1)} %bitcast.220) | data formatting | bytes 16777216 | tf_op jit(solution)/shard_map/while | solution.py:102
  64.9 11.7 %copy.95 = bf16[1,2,4096,512]{2,3,1,0:T(8,128)(2,1)} copy(bf16[1,2,4096,512]{3,2,1,0:T(8,128)(2,1)} %get-tuple-element.512) | data formatting | bytes 16777216
  76.6 19.0 %copy.69 = bf16[2,4096,8,64]{3,2,1,0:T(8,128)(2,1)} copy(bf16[2,4096,8,64]{1,3,2,0:T(8,128)(2,1)} %bitcast.221) | data formatting | bytes 16777216 | tf_op jit(solution)/shard_map/while | solution.py:102
  96.2 10.4 %fusion.59 = bf16[3,1026,512]{2,1,0:T(8,128)(2,1)S(1)} fusion(bf16[3,512,2048]{2,1,0:T(8,128)(2,1)} %all-gather.5.cloned.1.call-done, f32[2048]{0:T(1024)S(1)} %copy-done.10, f32[1026]{0:T(1024)S(1)} %add_rsqrt_fusion.1, bf16[2,2048]{1,0:T(2,128)(2,1)S(1)} %copy-done.4, bf16[1024,2048]{1,0:T(8,128)(2,1)} %param.20), kind=kOutput, calls=%fused_computation.96 | convolution fusion | flops 6471318528 | bytes 13658120 | tf_op jit(solution)/shard_map/td,kcd->ktc/dot_general | solution.py:36
  125.0 66.9 %while.52 = (s32[]{:T(128)}, f32[8,1]{0,1:T(1,128)S(1)}, f32[8,1]{0,1:T(1,128)S(1)}, f32[8,1,64]{2,1,0:T(1,128)S(1)}, s32[]{:T(128)}, /*index=5*/bf16[2,4096,8,6...) while((s32[]{:T(128)}, f32[8,1]{0,1:T(1,128)S(1)}, ...), condition=%wide.region_11.12_spmd, body=%wide.region_8.11_spmd.sunk | while | flops 1083422 | bytes 19995780 | solution.py:102
  125.0 6.5 fusion.138
  133.3 6.5 fusion.138
  141.7 6.5 fusion.138
  192.5 66.4 %while.53 = (s32[]{:T(128)}, f32[8,1]{0,1:T(1,128)S(1)}, f32[8,1]{0,1:T(1,128)S(1)}, f32[8,1,64]{2,1,0:T(1,128)S(1)}, s32[]{:T(128)}, /*index=5*/bf16[2,4096,8,6...) while((s32[]{:T(128)}, f32[8,1]{0,1:T(1,128)S(1)}, ...), condition=%wide.region_15.16_spmd, body=%wide.region_12.15_spmd.sunk | while | flops 1083422 | bytes 19995780 | solution.py:102
  192.5 6.5 fusion.147
  250.6 6.5 fusion.147
  284.5 13.6 %fusion.39 = (f32[8,1024]{1,0:T(8,128)S(1)}, f32[8,1024,1024]{1,2,0:T(8,128)}) fusion(pred[1024,1024]{0,1:T(8,128)(4,1)S(1)} %copy-done, bf16[1024,8,32]{0,2,1:T(8,128)(2,1)S(1)} %get-tuple-element.520, bf16[1024,8,32]{0,2,1:T(8,128)(2,1)S(1)} %get-tuple-element.521, bf16[1024,8,32]{0,2,1:T(8,128)(2,1)S(1)} %get-tuple-element.517, ...), kind=kOutput, calls=%fused_computation.66 | convolution fusion | flops 1103093760 | bytes 36732928 | tf_op jit(solution)/shard_map/qhd,khd->hqk/dot_general | solution.py:68
  298.1 14.3 %fusion.41 = f32[8,1024]{1,0:T(8,128)S(1)} fusion(f32[8,1024,1024]{1,2,0:T(8,128)} %get-tuple-element.545, f32[8,1024]{1,0:T(8,128)S(1)} %get-tuple-element.790, pred[1024,1024]{0,1:T(8,128)(4,1)S(1)} %copy-done), kind=kLoop, calls=%fused_computation.68 | loop fusion | flops 33546240 | bytes 34668544 | tf_op jit(solution)/shard_map/reduce_sum | solution.py:72
  312.4 16.0 %fusion.42 = f32[8,1024,64]{1,2,0:T(8,128)} fusion(bf16[1024,8,64]{0,2,1:T(8,128)(2,1)S(1)} %copy-done.3, f32[8,1024,1024]{1,2,0:T(8,128)} %get-tuple-element.545, f32[8,1024]{1,0:T(8,128)S(1)} %get-tuple-element.790, pred[1024,1024]{0,1:T(8,128)(4,1)S(1)} %copy-done), kind=kOutput, calls=%fused_computation.69 | convolution fusion | flops 1107296256 | bytes 37781504 | tf_op jit(solution)/shard_map/hqk,khd->hqd/dot_general | solution.py:73
  328.5 63.4 %while.51 = (s32[]{:T(128)}, f32[8,1024]{1,0:T(8,128)S(1)}, f32[8,1024]{1,0:T(8,128)S(1)}, f32[8,1024,64]{1,2,0:T(8,128)}, s32[]{:T(128)}, /*index=5*/bf16[2,204...) while((s32[]{:T(128)}, f32[8,1024]{1,0:T(8,128)S(1)}, ...), condition=%wide.region_7.8_spmd, body=%wide.region_4.7_spmd.sunk | while | flops 1120945152 | bytes 82315496 | solution.py:102
  400.7 14.4 %all-to-all-done.1 = bf16[8,128,512]{2,1,0:T(8,128)(2,1)S(1)} async-done(((bf16[8,128,512]{2,1,0:T(8,128)(2,1)}), bf16[8,128,512]{2,1,0:T(8,128)(2,1)S(1)}, u32[]{:S(2)}, u32[]{:S(2)}) %all-to-all-start.1) | async-done | bytes 1048608 | tf_op jit(solution)/shard_map/all_to_all | solution.py:180
  423.1 153.9 %all-reduce.3.cloned.1.call-done = bf16[1026,2048]{1,0:T(8,128)(2,1)} async-done(((bf16[1026,2048]{1,0:T(8,128)(2,1)}), bf16[1026,2048]{1,0:T(8,128)(2,1)}) %all-reduce.3.cloned.1.call-update) | async-done | bytes 4202512 | tf_op jit(solution)/shard_map/psum | solution.py:54
  581.5 89.4 %all-gather.9.cloned.1.call-done = bf16[2,2048,2048]{2,1,0:T(8,128)(2,1)} async-done(((bf16[2,2048,256]{2,1,0:T(8,128)(2,1)}), bf16[2,2048,2048]{2,1,0:T(8,128)(2,1)}) %all-gather.9.cloned.1.call-update) | async-done | bytes 16777232 | tf_op jit(solution)/shard_map/all_gather | solution.py:39
  670.9 25.3 %convolution_bitcast_fusion = f32[2,1026,2048]{2,1,0:T(8,128)} fusion(bf16[2,2048,2048]{2,1,0:T(8,128)(2,1)} %all-gather.9.cloned.1.call-done, bf16[1026,2048]{1,0:T(8,128)(2,1)} %all-reduce.3.cloned.1.call-done, f32[2048]{0:T(1024)S(1)} %copy-done.11, f32[1026]{0:T(1024)S(1)} %add_rsqrt_fusion, bf16[2,2048]{1,0:T(2,128)(2,1)S(1)} %copy-done.5, ...), kind=kOutput, calls=%fused_computation.71 | convolution fusion | flops 17232334848 | bytes 42004488 | tf_op jit(solution)/shard_map/td,kcd->ktc/dot_general | solution.py:36
  696.2 30.8 %all-gather.11.cloned.1.call-done = bf16[2048,2048]{1,0:T(8,128)(2,1)} async-done(((bf16[256,2048]{1,0:T(8,128)(2,1)}), bf16[2048,2048]{1,0:T(8,128)(2,1)}) %all-gather.11.cloned.1.call-update) | async-done | bytes 8388624 | tf_op jit(solution)/shard_map/all_gather | solution.py:48
  727.1 17.7 %convolution_convert_fusion = bf16[1026,2048]{1,0:T(8,128)(2,1)} fusion(bf16[2048,2048]{1,0:T(8,128)(2,1)} %all-gather.11.cloned.1.call-done, f32[2,1026,2048]{2,1,0:T(8,128)} %convolution_bitcast_fusion), kind=kOutput, calls=%fused_computation.85 | convolution fusion | flops 8621420544 | bytes 29401088 | tf_op jit(solution)/shard_map/tc,dc->td/dot_general | solution.py:45
  744.8 156.2 %all-reduce.5.cloned.1.call-done = bf16[1026,2048]{1,0:T(8,128)(2,1)} async-done(((bf16[1026,2048]{1,0:T(8,128)(2,1)}), bf16[1026,2048]{1,0:T(8,128)(2,1)}) %all-reduce.5.cloned.1.call-update) | async-done | bytes 4202512 | tf_op jit(solution)/shard_map/psum | solution.py:54
  (319 shorter events, 252.6 us)
Async XLA Ops:
  7.2 14.2 %copy-start.9 = (s32[16]{0:T(128)S(1)}, s32[16]{0:T(128)}, u32[]{:S(2)}) copy-start(s32[16]{0:T(128)} %param.31) | copy-start | bytes 196
  7.2 14.3 %copy-start.6 = (s32[2]{0:T(128)S(1)}, s32[2]{0:T(128)}, u32[]{:S(2)}) copy-start(s32[2]{0:T(128)} %param.33) | copy-start | bytes 28
  7.2 89.0 %all-gather.5.cloned.1.call-start = ((), (), s32[]{:S(2)}) async-start(), calls=%async_computation.4 | async-start | bytes 7077888 | tf_op jit(solution)/shard_map/all_gather | solution.py:39
  7.9 408.0 %all-gather.7.cloned.1.call-start = ((), (), s32[]{:S(2)}) async-start(), calls=%async_computation.5 | async-start | bytes 2359296 | tf_op jit(solution)/shard_map/all_gather | solution.py:48
  21.5 12.6 %copy-start.7 = (s32[2]{0:T(128)}, s32[2]{0:T(128)S(1)}, u32[]{:S(2)}) copy-start(s32[2]{0:T(128)S(1)} %get-tuple-element.494) | copy-start | bytes 28
  76.6 19.5 %copy-start.4 = (bf16[2,2048]{1,0:T(2,128)(2,1)S(1)}, bf16[2,2048]{1,0:T(2,128)(2,1)}, u32[]{:S(2)}) copy-start(bf16[2,2048]{1,0:T(2,128)(2,1)} %param.21) | copy-start | bytes 24580
  76.6 19.6 %copy-start.10 = (f32[2048]{0:T(1024)S(1)}, f32[2048]{0:T(1024)}, u32[]{:S(2)}) copy-start(f32[2048]{0:T(1024)} %param.22) | copy-start | bytes 24580
  107.5 11.9 %all-to-all-start.2 = ((bf16[3,8,2,512]{3,2,0,1:T(2,128)(2,1)}), bf16[3,8,2,512]{3,2,0,1:T(2,128)(2,1)S(1)}, u32[]{:S(2)}, u32[]{:S(2)}) async-start(bf16[3,8,2,512]{3,2,0,1:T(2,128)(2,1)} %broadcast_in_dim.223), calls=%async_computation.2 | async-start | bytes 98304 | tf_op jit(solution)/shard_map/all_to_all | solution.py:139
  119.4 140.7 %all-to-all-start = ((bf16[3,8,128,512]{3,2,0,1:T(8,128)(2,1)}), bf16[3,8,128,512]{3,2,0,1:T(8,128)(2,1)S(1)}, u32[]{:S(2)}, u32[]{:S(2)}) async-start(bf16[3,8,128,512]{3,2,0,1:T(8,128)(2,1)} %select_bitcast_fusion), calls=%async_computation | async-start | bytes 6291456 | tf_op jit(solution)/shard_map/all_to_all | solution.py:138
  192.5 66.8 %copy-start.8 = (s32[2]{0:T(128)S(1)}, s32[2]{0:T(128)}, u32[]{:S(2)}) copy-start(s32[2]{0:T(128)} %copy-done.7) | copy-start | bytes 28
  260.0 135.4 %all-to-all-start.3 = ((bf16[8,2,512]{2,1,0:T(2,128)(2,1)}), bf16[8,2,512]{2,1,0:T(2,128)(2,1)}, u32[]{:S(2)}, u32[]{:S(2)}) async-start(bf16[8,2,512]{2,1,0:T(2,128)(2,1)} %reshape.531), calls=%async_computation.3 | async-start | bytes 32768 | tf_op jit(solution)/shard_map/all_to_all | solution.py:181
  274.7 9.9 %copy-start = (pred[1024,1024]{0,1:T(8,128)(4,1)S(1)}, pred[1024,1024]{0,1:T(8,128)(4,1)}, u32[]{:S(2)}) copy-start(pred[1024,1024]{0,1:T(8,128)(4,1)} %iota_compare_fusion) | copy-start | bytes 3145732
  298.1 14.3 %copy-start.3 = (bf16[1024,8,64]{0,2,1:T(8,128)(2,1)S(1)}, bf16[1024,8,64]{0,2,1:T(8,128)(2,1)}, u32[]{:S(2)}) copy-start(bf16[1024,8,64]{0,2,1:T(8,128)(2,1)} %reshape_squeeze.8) | copy-start | bytes 3145732
  335.3 3.9 copy-start.1
  351.1 3.9 copy-start.1
  366.9 3.9 copy-start.1
  391.9 7.9 copy-start.12
  395.5 19.6 %all-to-all-start.1 = ((bf16[8,128,512]{2,1,0:T(8,128)(2,1)}), bf16[8,128,512]{2,1,0:T(8,128)(2,1)S(1)}, u32[]{:S(2)}, u32[]{:S(2)}) async-start(bf16[8,128,512]{2,1,0:T(8,128)(2,1)} %copy.64), calls=%async_computation.1 | async-start | bytes 2097152 | tf_op jit(solution)/shard_map/all_to_all | solution.py:180
  399.7 177.3 %all-reduce.3.cloned.1.call-start = ((), (), s32[]{:S(2)}) async-start(), calls=%async_computation.6 | async-start | bytes 8454144 | tf_op jit(solution)/shard_map/psum | solution.py:54
  415.9 161.1 %copy-start.5 = (bf16[2,2048]{1,0:T(2,128)(2,1)S(1)}, bf16[2,2048]{1,0:T(2,128)(2,1)}, u32[]{:S(2)}) copy-start(bf16[2,2048]{1,0:T(2,128)(2,1)} %param.21) | copy-start | bytes 24580
  421.9 249.0 %copy-start.11 = (f32[2048]{0:T(1024)S(1)}, f32[2048]{0:T(1024)}, u32[]{:S(2)}) copy-start(f32[2048]{0:T(1024)} %param.23) | copy-start | bytes 24580
  421.9 249.0 %all-gather.9.cloned.1.call-start = ((), (), s32[]{:S(2)}) async-start(), calls=%async_computation.7 | async-start | bytes 18874368 | tf_op jit(solution)/shard_map/all_gather | solution.py:39
  422.5 304.6 %all-gather.11.cloned.1.call-start = ((), (), s32[]{:S(2)}) async-start(), calls=%async_computation.8 | async-start | bytes 9437184 | tf_op jit(solution)/shard_map/all_gather | solution.py:48
  423.1 477.9 %all-reduce.5.cloned.1.call-start = ((), (), s32[]{:S(2)}) async-start(), calls=%async_computation.9 | async-start | bytes 8454144 | tf_op jit(solution)/shard_map/psum | solution.py:54
  (5 other events, 9.2 us)
Sparse Core Ops, SparseCore 0:
  9.9 49.3 all-gather.4
  61.2 27.9 all-gather.6
  422.0 154.9 all-reduce.2
  578.7 92.1 all-gather.8
  672.6 54.3 all-gather.10
  744.9 156.0 all-reduce.4
where the time goes:
time: 928 us; the launch traced here: 917 us
  waiting for transfers between devices  447 us (48%)
  local copies, waits for them, and re-layouts  227 us (24%)
  matrix products  129 us (14%)
  other arithmetic  77.8 us (8%)
  starting transfers between devices  18.7 us (2%)
  between operations  16.7 us (2%)
    psum x2, waiting for transfers between devices, over_heads(): lax.psum(partial_value.astype(jnp.bfloat16), 'head').astype(jnp.float32)  310 us
    slice x20, local copies, waits for them, and re-layouts, one_block(): values_block = lax.dynamic_slice_in_dim(cached[1], begin, BLOCK, 0)  115 us
    all_gather x2, waiting for transfers between devices, fold_rows(): lax.all_gather(weights, 'tok', axis=2, tiled=True)  89.4 us
    while x2, local copies, waits for them, and re-layouts, attend_local(): lax.fori_loop(0, block_count, one_block, (top, total, mixed))  37.9 us
    dot_general x2, matrix products, fold_rows(): jnp.einsum('td,kcd->ktc', inputs, lax.all_gather(weights, 'tok', axis=2,...  35.7 us
    all_gather x2, waiting for transfers between devices, map_rows(): lax.all_gather(weights, 'tok', axis=0, tiled=True)  30.8 us
    unnamed x26, local copies, waits for them, and re-layouts  29.5 us
    dot_general x2, matrix products, map_rows(): jnp.einsum('tc,dc->td', inputs, lax.all_gather(weights, 'tok', axis=0, ti...  23.6 us
  transfers between devices with their start and end apart: 10, of which 5 were waited for; matrix products, arithmetic and copies ran while one was open for 43% of the time, Pallas kernels for 0%

commit v1 on v0

v1 whole, which is shorter than its diff:
```python
import jax
import jax.numpy as jnp
from jax import lax
from jax.experimental import pallas as pl
from jax.experimental.pallas import tpu as pltpu
from jax.sharding import PartitionSpec as P

HD = 64
Q_ROWS = 512
K_ROWS = 512
DEC_ROWS = 1024


rope_base = 130000.0
norm_eps = 1e-05
masked_score = -1e30


def rotate(values, positions):
    width = values.shape[-1]
    half = width // 2
    freqs = rope_base ** (-(jnp.arange(half, dtype=jnp.float32) * 2.0 / width))
    angles = positions.astype(jnp.float32)[:, None] * freqs[None, :]
    cosine = jnp.cos(angles)[:, None, :]
    sine = jnp.sin(angles)[:, None, :]
    first = values[..., :half]
    second = values[..., half:]
    return jnp.concatenate(
        [first * cosine - second * sine, second * cosine + first * sine], axis=-1
    )


def rms_norm(rows, gain):
    rows = rows.astype(jnp.float32)
    factor = lax.rsqrt(jnp.mean(rows * rows, axis=-1, keepdims=True) + norm_eps)
    return (rows * factor * gain).astype(jnp.bfloat16)


def fold_rows(inputs, weights):
    return jnp.einsum("td,kcd->ktc", inputs, weights, preferred_element_type=jnp.float32)


def map_rows(inputs, weights):
    return jnp.einsum("tc,dc->td", inputs, weights, preferred_element_type=jnp.float32)


def whole(weights, axis):
    return lax.all_gather(weights, "tok", axis=axis, tiled=True)


def over_heads(partial_value):
    return lax.psum(partial_value.astype(jnp.bfloat16), "head").astype(jnp.float32)


def rope_tables(positions, width):
    half = HD // 2
    freqs = rope_base ** (-(jnp.arange(half, dtype=jnp.float32) * 2.0 / HD))
    angles = positions.astype(jnp.float32)[:, None] * freqs[None, :]
    cosine = jnp.cos(angles)
    sine = jnp.sin(angles)
    copies = width // HD
    return (
        jnp.tile(jnp.concatenate([cosine, cosine], axis=1), (1, copies)),
        jnp.tile(jnp.concatenate([-sine, sine], axis=1), (1, copies)),
    )


def swap_halves(values):
    half = HD // 2
    width = values.shape[-1]
    lane = lax.broadcasted_iota(jnp.int32, values.shape, values.ndim - 1)
    axis = values.ndim - 1
    return jnp.where(
        lane % HD < half,
        pltpu.roll(values, width - half, axis),
        pltpu.roll(values, half, axis),
    )


def prefill_kernel(
    limit_ref, q_ref, k_ref, v_ref, cos_ref, sin_ref, cache_ref, out_ref, q_rot, k_rot, v_ext, c_ext
):
    span = q_ref.shape[1]
    length = cache_ref.shape[2]
    pair = q_ref.shape[2]
    limit = limit_ref[0]
    cosine = cos_ref[...]
    sine = sin_ref[...]
    lane = lax.broadcasted_iota(jnp.int32, (1, pair), 1)
    halves = (lane < HD, lane >= HD)

    key = k_ref[0].astype(jnp.float32)
    k_rot[...] = (key * cosine + swap_halves(key) * sine).astype(jnp.bfloat16)
    query = q_ref[0].astype(jnp.float32)
    query = (query * cosine + swap_halves(query) * sine).astype(jnp.bfloat16)
    query = query * jnp.bfloat16(HD**-0.5)
    one = jnp.ones((), jnp.bfloat16)
    zero = jnp.zeros((), jnp.bfloat16)
    for side in range(2):
        q_rot[side] = jnp.where(halves[side], query, zero)
        v_ext[side] = jnp.where(halves[side], v_ref[0], one)
        c_ext[side] = jnp.where(halves[side], cache_ref[0, 1], one)

    def score(rows, keys):
        return lax.dot_general(
            rows, keys, (((1,), (1,)), ((), ())), preferred_element_type=jnp.float32
        )

    def fold(state, scores, values):
        top, mixed = state
        new_top = jnp.maximum(top, jnp.max(scores, axis=-1, keepdims=True))
        weights = jnp.exp(scores - new_top).astype(jnp.bfloat16)
        factor = jnp.exp(top - new_top)
        return new_top, mixed * factor + jnp.dot(
            weights, values, preferred_element_type=jnp.float32
        )

    for block in range(span // Q_ROWS):
        start = block * Q_ROWS
        rows = [q_rot[side, start : start + Q_ROWS, :] for side in range(2)]
        keys = k_rot[start : start + Q_ROWS, :]
        shape = (Q_ROWS, Q_ROWS)
        seen = lax.broadcasted_iota(jnp.int32, shape, 1) <= lax.broadcasted_iota(
            jnp.int32, shape, 0
        )
        states = []
        for side in range(2):
            scores = jnp.where(seen, score(rows[side], keys), masked_score)
            top = jnp.max(scores, axis=-1, keepdims=True)
            weights = jnp.exp(scores - top).astype(jnp.bfloat16)
            mixed = jnp.dot(
                weights,
                v_ext[side, start : start + Q_ROWS, :],
                preferred_element_type=jnp.float32,
            )
            states.append((top, mixed))
        for earlier in range(block):
            begin = earlier * Q_ROWS
            keys = k_rot[begin : begin + Q_ROWS, :]
            for side in range(2):
                states[side] = fold(
                    states[side],
                    score(rows[side], keys),
                    v_ext[side, begin : begin + Q_ROWS, :],
                )

        def cached(index, state, masked):
            begin = pl.multiple_of(index * K_ROWS, K_ROWS)
            keys_now = cache_ref[0, 0, pl.ds(begin, K_ROWS), :]
            result = []
            for side in range(2):
                scores = score(rows[side], keys_now)
                if masked:
                    spot = begin + lax.broadcasted_iota(jnp.int32, (1, K_ROWS), 1)
                    scores = jnp.where(spot < limit, scores, masked_score)
                result.append(
                    fold(state[side], scores, c_ext[side, pl.ds(begin, K_ROWS), :])
                )
            return tuple(result)

        full = limit // K_ROWS
        every = (limit + K_ROWS - 1) // K_ROWS
        states = lax.fori_loop(0, full, lambda i, s: cached(i, s, False), tuple(states))
        states = lax.fori_loop(full, every, lambda i, s: cached(i, s, True), states)
        parts = []
        for side in range(2):
            mixed = states[side][1]
            total = pltpu.roll(mixed, HD, 1)
            parts.append(mixed / total)
        out_ref[start : start + Q_ROWS, :] = jnp.where(halves[0], parts[0], parts[1]).astype(
            jnp.bfloat16
        )


def prefill_attend(qkv, offset, cache):
    _, span, width = qkv.shape
    length = cache.shape[2]
    pair = 2 * HD
    cosine, sine = rope_tables(offset + jnp.arange(span, dtype=jnp.int32), pair)
    part = lambda which: pl.BlockSpec((1, span, pair), lambda p, limit: (which, 0, p))
    table = pl.BlockSpec((span, pair), lambda p, limit: (0, 0))
    return pl.pallas_call(
        prefill_kernel,
        out_shape=jax.ShapeDtypeStruct((span, width), jnp.bfloat16),
        grid_spec=pltpu.PrefetchScalarGridSpec(
            num_scalar_prefetch=1,
            grid=(width // pair,),
            in_specs=[
                part(0),
                part(1),
                part(2),
                table,
                table,
                pl.BlockSpec((1, 2, length, pair), lambda p, limit: (0, 0, 0, p)),
            ],
            out_specs=pl.BlockSpec((span, pair), lambda p, limit: (0, p)),
            scratch_shapes=[
                pltpu.VMEM((2, span, pair), jnp.bfloat16),
                pltpu.VMEM((span, pair), jnp.bfloat16),
                pltpu.VMEM((2, span, pair), jnp.bfloat16),
                pltpu.VMEM((2, length, pair), jnp.bfloat16),
            ],
        ),
        compiler_params=pltpu.CompilerParams(vmem_limit_bytes=40 * 1024 * 1024),
        cost_estimate=pl.CostEstimate(
            flops=16 * span * 3 * span * width,
            bytes_accessed=4 * length * width + 8 * span * width,
            transcendentals=span * 3 * span * width // HD,
        ),
        name="prefill_attend",
    )(offset[None], qkv, qkv, qkv, cosine, sine, cache)


def decode_kernel(limits_ref, q_ref, k_ref, v_ref, cache_ref, out_ref, top_ref, total_ref, mixed_ref):
    request = pl.program_id(0)
    index = pl.program_id(1)
    limit = limits_ref[request]
    heads, width = q_ref.shape[1:]
    block = cache_ref.shape[2]

    @pl.when(index == 0)
    def _():
        own = q_ref[0].astype(jnp.float32) * k_ref[0].astype(jnp.float32)
        top_ref[...] = jnp.sum(own, axis=-1, keepdims=True)
        total_ref[...] = jnp.ones_like(total_ref)
        mixed_ref[...] = jnp.broadcast_to(v_ref[0].astype(jnp.float32), (heads, width))

    @pl.when(index * block < limit)
    def _():
        scores = lax.dot_general(
            q_ref[0],
            cache_ref[0, 0],
            (((1,), (1,)), ((), ())),
            preferred_element_type=jnp.float32,
        )
        spot = index * block + lax.broadcasted_iota(jnp.int32, (1, block), 1)
        scores = jnp.where(spot < limit, scores, masked_score)
        top = top_ref[...]
        new_top = jnp.maximum(top, jnp.max(scores, axis=-1, keepdims=True))
        weights = jnp.exp(scores - new_top)
        factor = jnp.exp(top - new_top)
        top_ref[...] = new_top
        total_ref[...] = total_ref[...] * factor + jnp.sum(weights, axis=-1, keepdims=True)
        mixed_ref[...] = mixed_ref[...] * factor + jnp.dot(
            weights.astype(jnp.bfloat16), cache_ref[0, 1], preferred_element_type=jnp.float32
        )

    @pl.when(index == pl.num_programs(1) - 1)
    def _():
        shape = (heads, width)
        mine = lax.broadcasted_iota(jnp.int32, shape, 1) // HD == lax.broadcasted_iota(
            jnp.int32, shape, 0
        )
        value = jnp.where(mine, mixed_ref[...] / total_ref[...], 0.0)
        out_ref[0] = jnp.sum(value, axis=0, keepdims=True).astype(jnp.bfloat16)


def decode_attend(qkv, lengths, cache):
    _, count, width = qkv.shape
    heads = width // HD
    block = min(DEC_ROWS, cache.shape[2])
    split = qkv.reshape(3, count, heads, HD)
    q_rot = rotate(split[0].astype(jnp.float32), lengths).astype(jnp.bfloat16)
    k_rot = rotate(split[1].astype(jnp.float32), lengths).astype(jnp.bfloat16)
    q_rot = q_rot * jnp.bfloat16(HD**-0.5)
    spread = jnp.where(
        jnp.eye(heads, dtype=jnp.bool_)[None, :, :, None], q_rot[:, None], jnp.bfloat16(0)
    ).reshape(count, heads, width)

    def cache_at(request, index, limits):
        last = (limits[request] - 1) // block
        return (request, 0, jnp.minimum(index, last), 0)

    row = pl.BlockSpec((1, 1, width), lambda request, index, limits: (request, 0, 0))
    return pl.pallas_call(
        decode_kernel,
        out_shape=jax.ShapeDtypeStruct((count, 1, width), jnp.bfloat16),
        grid_spec=pltpu.PrefetchScalarGridSpec(
            num_scalar_prefetch=1,
            grid=(count, cache.shape[2] // block),
            in_specs=[
                pl.BlockSpec((1, heads, width), lambda request, index, limits: (request, 0, 0)),
                row,
                row,
                pl.BlockSpec((1, 2, block, width), cache_at),
            ],
            out_specs=row,
            scratch_shapes=[
                pltpu.VMEM((heads, 1), jnp.float32),
                pltpu.VMEM((heads, 1), jnp.float32),
                pltpu.VMEM((heads, width), jnp.float32),
            ],
        ),
        compiler_params=pltpu.CompilerParams(vmem_limit_bytes=32 * 1024 * 1024),
        cost_estimate=pl.CostEstimate(
            flops=4 * count * heads * cache.shape[2] * width,
            bytes_accessed=4 * count * cache.shape[2] * width,
            transcendentals=count * cache.shape[2] * heads,
        ),
        name="decode_attend",
    )(lengths, spread, k_rot.reshape(count, 1, width), qkv[2].reshape(count, 1, width), cache)[:, 0]


def on_device(
    pre_tokens,
    dec_tokens,
    attn_gain,
    mlp_gain,
    w_qkv,
    w_out,
    w_gate_up,
    w_down,
    pre_cache,
    dec_cache,
    pre_order,
    dec_order,
    pre_offsets,
    dec_lengths,
):
    tok_count = lax.axis_size("tok")
    tok_index = lax.axis_index("tok")
    span_rows = pre_tokens.shape[0]
    piece_len = span_rows // tok_count
    dec_local = dec_tokens.shape[0]
    dec_total = dec_order.shape[0]
    group_width = w_qkv.shape[1]
    rows = jnp.concatenate([pre_tokens, dec_tokens], axis=0)
    normed = rms_norm(rows, attn_gain)
    projected = fold_rows(normed, whole(w_qkv, 2)).astype(jnp.bfloat16)
    pre_part = projected[:, :span_rows].reshape(3, tok_count, piece_len, group_width)
    pre_send = jnp.take(pre_part, pre_order, axis=1)
    dec_part = projected[:, span_rows:]
    dec_send = jnp.broadcast_to(dec_part[:, None], (3, tok_count, dec_local, group_width))
    pre_recv, dec_recv = (
        lax.all_to_all(pre_send, "tok", split_axis=1, concat_axis=1, tiled=True),
        lax.all_to_all(dec_send, "tok", split_axis=1, concat_axis=1, tiled=True),
    )
    pre_recv = pre_recv.reshape(3, span_rows, group_width)
    dec_recv = dec_recv.reshape(3, dec_total, group_width)
    offset_now = pre_offsets[0]
    pre_att = prefill_attend(pre_recv, offset_now, pre_cache)
    pre_att, out_full, gate_up_full, down_full = lax.optimization_barrier(
        (pre_att, whole(w_out, 0), whole(w_gate_up, 2), whole(w_down, 0))
    )
    own_slots = lax.dynamic_slice_in_dim(dec_order, tok_index * dec_local, dec_local)
    dec_mine = jnp.take(dec_recv, own_slots, axis=1)
    dec_att = decode_attend(dec_mine, dec_lengths, dec_cache)
    picker = (jnp.arange(dec_total, dtype=jnp.int32)[:, None] == own_slots[None, :]).astype(
        jnp.bfloat16
    )
    dec_back = (
        jnp.dot(picker, dec_att, preferred_element_type=jnp.float32)
        .astype(jnp.bfloat16)
        .reshape(tok_count, dec_local, group_width)
    )
    pre_back = pre_att.reshape(tok_count, piece_len, group_width)
    pre_ret, dec_ret = (
        lax.all_to_all(pre_back, "tok", split_axis=0, concat_axis=0, tiled=True),
        lax.all_to_all(dec_back, "tok", split_axis=0, concat_axis=0, tiled=True),
    )
    slot_range = jnp.arange(tok_count, dtype=jnp.int32)
    inverse = jnp.sum(
        jnp.where(pre_order[None, :] == slot_range[:, None], slot_range[None, :], 0), axis=1
    )
    pre_mixed = jnp.take(pre_ret, inverse, axis=0).reshape(span_rows, group_width)
    dec_mixed = jnp.sum(dec_ret.astype(jnp.float32), axis=0).astype(jnp.bfloat16)
    attended = jnp.concatenate([pre_mixed, dec_mixed], axis=0)
    resid = rows.astype(jnp.float32) + over_heads(map_rows(attended, out_full))
    mlp_in = rms_norm(resid, mlp_gain)
    gate_up = fold_rows(mlp_in, gate_up_full)
    hidden = (jax.nn.silu(gate_up[0]) * gate_up[1]).astype(jnp.bfloat16)
    final = (resid + over_heads(map_rows(hidden, down_full))).astype(jnp.bfloat16)
    return (final[:span_rows], final[span_rows:])


def solution(mesh):
    placed = (
        P("tok", None),
        P("tok", None),
        P(),
        P(),
        P(None, "head", "tok"),
        P("tok", "head"),
        P(None, "head", "tok"),
        P("tok", "head"),
        P("tok", None, None, "head"),
        P("tok", None, None, "head"),
        P(),
        P(),
        P("tok"),
        P("tok"),
    )
    return jax.shard_map(
        on_device,
        mesh=mesh,
        in_specs=placed,
        out_specs=(P("tok", None), P("tok", None)),
        check_vma=False,
    )
```

time: 928 us -> 657 us (0.71); the launches traced: 917 us -> 656 us
  local copies, waits for them, and re-layouts: 227 us -> 20.9 us
  matrix products: 129 us -> 54.5 us
  Pallas kernels: 0 us -> 58.1 us
  other arithmetic: 77.8 us -> 20.5 us
  waiting for transfers between devices: 447 us -> 472 us
    slice x23 -> x0, local copies, waits for them, and re-layouts: 129 us -> none  [the longest x20 115 us: one_block(): values_block = lax.dynamic_slice_in_dim(cached[1], begin, BLOCK, 0)]
    dot_general x46 -> x4, matrix products: 128 us -> 54.4 us  [the longest x2 34 us: fold_rows(): jnp.einsum('td,kcd->ktc', inputs, weights, preferred_element_type=jnp.flo...]
    pallas_call x0 -> x2, Pallas kernels: none -> 58.1 us  [the longest x1 52.6 us: prefill_attend(): pl.pallas_call(prefill_kernel, out_shape=jax.ShapeDtypeStruct((span, widt...]
    while x38 -> x0, local copies, waits for them, and re-layouts: 43.2 us -> none  [the longest x2 37.9 us: attend_local(): lax.fori_loop(0, block_count, one_block, (top, total, mixed))]
    all_to_all x1, waiting for transfers between devices: 0.01 us -> 33.5 us  [on_device(): lax.all_to_all(pre_send, 'tok', split_axis=1, concat_axis=1, tiled=True)]
    reduce_sum x5 -> x0, other arithmetic: 29.8 us -> none  [the longest x4 15.5 us: one_block(): total_next = total_now * factor + jnp.sum(block_weights, axis=-1)]
    unnamed x26 -> x24, local copies, waits for them, and re-layouts: 29.5 us -> 8.59 us
    lt x20 -> x0, other arithmetic: 12.6 us -> none  [one_block(): live = begin + jnp.arange(BLOCK, dtype=jnp.int32) < limit]
  transfers between devices with their start and end apart: 10 -> 10, of which waited for: 5 -> 6; matrix products, arithmetic and copies ran while one was open for 43% -> 4% of each run, Pallas kernels for 0% -> 9%
where the time goes in v1:
time: 657 us; the launch traced here: 656 us
  waiting for transfers between devices  472 us (72%)
  Pallas kernels  58.1 us (9%)
  matrix products  54.5 us (8%)
  local copies, waits for them, and re-layouts  20.9 us (3%)
  other arithmetic  20.5 us (3%)
  starting transfers between devices  15.4 us (2%)
  between operations  15.1 us (2%)
    psum x2, waiting for transfers between devices, over_heads(): lax.psum(partial_value.astype(jnp.bfloat16), 'head').astype(jnp.float32)  310 us
    all_gather x4, waiting for transfers between devices, whole(): return lax.all_gather(weights, 'tok', axis=axis, tiled=True)  110 us
    pallas_call x1, Pallas kernels, prefill_attend(): pl.pallas_call(prefill_kernel, out_shape=jax.ShapeDtypeStruct((span, widt...  52.6 us
    dot_general x2, matrix products, fold_rows(): jnp.einsum('td,kcd->ktc', inputs, weights, preferred_element_type=jnp.flo...  34 us
    all_to_all x1, waiting for transfers between devices, on_device(): lax.all_to_all(pre_send, 'tok', split_axis=1, concat_axis=1, tiled=True)  33.5 us
    dot_general x2, matrix products, map_rows(): jnp.einsum('tc,dc->td', inputs, weights, preferred_element_type=jnp.float32)  20.4 us
    all_to_all x1, waiting for transfers between devices, on_device(): lax.all_to_all(pre_back, 'tok', split_axis=0, concat_axis=0, tiled=True)  15 us
  transfers between devices with their start and end apart: 10, of which 6 were waited for; matrix products, arithmetic and copies ran while one was open for 4% of the time, Pallas kernels for 9%

profile of v1, /device:TPU:0, one launch (start us, length us, event | category | flops | bytes accessed | tf_op | source)
XLA Modules:
  0.0 656.3 jit_solution(17442820706006731499)
XLA Ops:
  11.3 3.1 fusion
  14.4 44.9 %all-gather.5.cloned.1.call-done = bf16[3,512,2048]{2,1,0:T(8,128)(2,1)} async-done(((bf16[3,512,256]{2,1,0:T(8,128)(2,1)}), bf16[3,512,2048]{2,1,0:T(8,128)(2,1)}) %all-gather.5.cloned.1.call-update) | async-done | bytes 6291472 | tf_op jit(solution)/shard_map/all_gather | solution.py:48
  59.3 10.4 %fusion.14 = bf16[3,1026,512]{2,1,0:T(8,128)(2,1)S(1)} fusion(bf16[3,512,2048]{2,1,0:T(8,128)(2,1)} %all-gather.5.cloned.1.call-done, f32[2048]{0:T(1024)S(1)} %copy-done.7, f32[1026]{0:T(1024)S(1)} %add_rsqrt_fusion.1, bf16[2,2048]{1,0:T(2,128)(2,1)S(1)} %copy-done.5, bf16[1024,2048]{1,0:T(8,128)(2,1)} %param.14), kind=kOutput, calls=%fused_computation.27 | convolution fusion | flops 6471318528 | bytes 13658120 | tf_op jit(solution)/shard_map/td,kcd->ktc/dot_general | solution.py:40
  70.6 3.3 all-to-all-start.2
  73.9 2.4 gather_fusion
  76.3 3.9 select_bitcast_fusion
  80.3 4.6 all-to-all-start
  88.4 5.8 copy-done
  94.2 5.5 decode_attend.1
  100.5 33.5 %all-to-all-done = bf16[3,8,128,512]{3,2,0,1:T(8,128)(2,1)} async-done(((bf16[3,8,128,512]{3,2,0,1:T(8,128)(2,1)}), bf16[3,8,128,512]{3,2,0,1:T(8,128)(2,1)}, u32[]{:S(2)}, u32[]{:S(2)}) %all-to-all-start) | async-done | bytes 3145760 | tf_op jit(solution)/shard_map/all_to_all | solution.py:335
  134.0 3.5 all-to-all-start.3
  137.5 3.2 copy.28
  142.0 52.6 %prefill_attend.1 = bf16[1024,512]{1,0:T(8,128)(2,1)} custom-call(s32[1]{0:T(128)} %copy.41.limit_ref, bf16[3,1024,512]{2,1,0:T(8,128)(2,1)S(1)} %bitcast.61, bf16[3,1024,512]{2,1,0:T(8,128)(2,1)S(1)} %bitcast.62, bf16[3,1024,512]{2,1,0:T(8,128)(2,1)S(1)} %bitcast.63, f32[1024,128]{1,0:T(8,128)S(1)} %copy.29.cos_ref, f32[1024,128]{1,0:T(8,128)S(1)} %copy.30.sin_ref, ...), custom_call_target="tpu_custom_call" | custom-call | flops 25769803776 | bytes 8388608 | tf_op jit(solution)/shard_map/prefill_attend/pallas_call | solution.py:182
  194.6 65.4 %all-gather.9.cloned.1.call-done = bf16[2,2048,2048]{2,1,0:T(8,128)(2,1)} async-done(((bf16[2,2048,256]{2,1,0:T(8,128)(2,1)}), bf16[2,2048,2048]{2,1,0:T(8,128)(2,1)}) %all-gather.9.cloned.1.call-update) | async-done | bytes 16777232 | tf_op jit(solution)/shard_map/all_gather | solution.py:48
  260.0 3.6 all-to-all-start.1
  263.9 15.0 %all-to-all-done.1 = bf16[8,128,512]{2,1,0:T(8,128)(2,1)S(1)} async-done(((bf16[8,128,512]{2,1,0:T(8,128)(2,1)}), bf16[8,128,512]{2,1,0:T(8,128)(2,1)S(1)}, u32[]{:S(2)}, u32[]{:S(2)}) %all-to-all-start.1) | async-done | bytes 1048608 | tf_op jit(solution)/shard_map/all_to_all | solution.py:358
  279.8 5.9 convolution_convert_fusion.1
  286.0 155.0 %all-reduce.3.cloned.1.call-done = bf16[1026,2048]{1,0:T(8,128)(2,1)} async-done(((bf16[1026,2048]{1,0:T(8,128)(2,1)}), bf16[1026,2048]{1,0:T(8,128)(2,1)}) %all-reduce.3.cloned.1.call-update) | async-done | bytes 4202512 | tf_op jit(solution)/shard_map/psum | solution.py:52
  441.1 4.4 multiply_reduce_fusion
  447.0 23.7 %convolution_bitcast_fusion = f32[2,1026,2048]{2,1,0:T(8,128)} fusion(bf16[2,2048,2048]{2,1,0:T(8,128)(2,1)} %all-gather.9.cloned.1.call-done, bf16[1026,2048]{1,0:T(8,128)(2,1)S(1)} %copy-done.4, f32[2048]{0:T(1024)S(1)} %copy-done.8, f32[1026]{0:T(1024)S(1)} %add_rsqrt_fusion, bf16[2,2048]{1,0:T(2,128)(2,1)S(1)} %copy-done.5, ...), kind=kOutput, calls=%fused_computation.3 | convolution fusion | flops 17232334848 | bytes 42004488 | tf_op jit(solution)/shard_map/td,kcd->ktc/dot_general | solution.py:40
  470.7 14.4 %convolution_convert_fusion = bf16[1026,2048]{1,0:T(8,128)(2,1)} fusion(bf16[2048,2048]{1,0:T(8,128)(2,1)S(1)} %bitcast.69, f32[2,1026,2048]{2,1,0:T(8,128)} %convolution_bitcast_fusion), kind=kOutput, calls=%fused_computation.17 | convolution fusion | flops 8621420544 | bytes 29401088 | tf_op jit(solution)/shard_map/tc,dc->td/dot_general | solution.py:44
  485.1 155.2 %all-reduce.5.cloned.1.call-done = bf16[1026,2048]{1,0:T(8,128)(2,1)} async-done(((bf16[1026,2048]{1,0:T(8,128)(2,1)}), bf16[1026,2048]{1,0:T(8,128)(2,1)}) %all-reduce.5.cloned.1.call-update) | async-done | bytes 4202512 | tf_op jit(solution)/shard_map/psum | solution.py:52
  640.3 6.2 add_convert_fusion
  647.1 2.3 slice.71
  (88 shorter events, 13.3 us)
Async XLA Ops:
  7.2 52.1 %copy-start.5 = (bf16[2,2048]{1,0:T(2,128)(2,1)S(1)}, bf16[2,2048]{1,0:T(2,128)(2,1)}, u32[]{:S(2)}) copy-start(bf16[2,2048]{1,0:T(2,128)(2,1)} %param.15) | copy-start | bytes 24580
  7.2 52.1 %copy-start.7 = (f32[2048]{0:T(1024)S(1)}, f32[2048]{0:T(1024)}, u32[]{:S(2)}) copy-start(f32[2048]{0:T(1024)} %param.16) | copy-start | bytes 24580
  7.2 52.1 %all-gather.5.cloned.1.call-start = ((), (), s32[]{:S(2)}) async-start(), calls=%async_computation.4 | async-start | bytes 7077888 | tf_op jit(solution)/shard_map/all_gather | solution.py:48
  7.9 186.7 %all-gather.7.cloned.1.call-start = ((), (), s32[]{:S(2)}) async-start(), calls=%async_computation.5 | async-start | bytes 2359296 | tf_op jit(solution)/shard_map/all_gather | solution.py:48
  8.7 186.0 %all-gather.11.cloned.1.call-start = ((), (), s32[]{:S(2)}) async-start(), calls=%async_computation.7 | async-start | bytes 9437184 | tf_op jit(solution)/shard_map/all_gather | solution.py:48
  9.4 250.6 %all-gather.9.cloned.1.call-start = ((), (), s32[]{:S(2)}) async-start(), calls=%async_computation.6 | async-start | bytes 18874368 | tf_op jit(solution)/shard_map/all_gather | solution.py:48
  70.6 9.7 %all-to-all-start.2 = ((bf16[3,8,2,512]{3,2,0,1:T(2,128)(2,1)}), bf16[3,8,2,512]{3,2,0,1:T(2,128)(2,1)S(1)}, u32[]{:S(2)}, u32[]{:S(2)}) async-start(bf16[3,8,2,512]{3,2,0,1:T(2,128)(2,1)} %broadcast_in_dim.114), calls=%async_computation.2 | async-start | bytes 98304 | tf_op jit(solution)/shard_map/all_to_all | solution.py:336
  76.3 9.2 %copy-start.1 = (s32[2]{0:T(128)S(1)}, s32[2]{0:T(128)}, u32[]{:S(2)}) copy-start(s32[2]{0:T(128)} %limits_ref.1) | copy-start | bytes 28
  80.3 6.6 %copy-start.6 = (s32[16]{0:T(128)S(1)}, s32[16]{0:T(128)}, u32[]{:S(2)}) copy-start(s32[16]{0:T(128)} %param.25) | copy-start | bytes 196
  80.3 53.7 %all-to-all-start = ((bf16[3,8,128,512]{3,2,0,1:T(8,128)(2,1)}), bf16[3,8,128,512]{3,2,0,1:T(8,128)(2,1)}, u32[]{:S(2)}, u32[]{:S(2)}) async-start(bf16[3,8,128,512]{3,2,0,1:T(8,128)(2,1)} %select_bitcast_fusion), calls=%async_computation | async-start | bytes 6291456 | tf_op jit(solution)/shard_map/all_to_all | solution.py:335
  88.4 5.8 copy-start
  134.0 126.0 %all-to-all-start.3 = ((bf16[8,2,512]{2,1,0:T(2,128)(2,1)}), bf16[8,2,512]{2,1,0:T(2,128)(2,1)S(1)}, u32[]{:S(2)}, u32[]{:S(2)}) async-start(bf16[8,2,512]{2,1,0:T(2,128)(2,1)} %reshape.189), calls=%async_computation.3 | async-start | bytes 32768 | tf_op jit(solution)/shard_map/all_to_all | solution.py:359
  137.5 4.5 copy-start.2
  142.0 121.6 %copy-start.9 = (s32[8]{0:T(128)S(1)}, s32[8]{0:T(128)}, u32[]{:S(2)}) copy-start(s32[8]{0:T(128)} %param.24) | copy-start | bytes 100
  260.0 18.9 %all-to-all-start.1 = ((bf16[8,128,512]{2,1,0:T(8,128)(2,1)}), bf16[8,128,512]{2,1,0:T(8,128)(2,1)S(1)}, u32[]{:S(2)}, u32[]{:S(2)}) async-start(bf16[8,128,512]{2,1,0:T(8,128)(2,1)} %bitcast.9), calls=%async_computation.1 | async-start | bytes 2097152 | tf_op jit(solution)/shard_map/all_to_all | solution.py:358
  263.6 177.5 %all-reduce.3.cloned.1.call-start = ((), (), s32[]{:S(2)}) async-start(), calls=%async_computation.8 | async-start | bytes 8454144 | tf_op jit(solution)/shard_map/psum | solution.py:52
  285.7 159.7 %copy-start.8 = (f32[2048]{0:T(1024)S(1)}, f32[2048]{0:T(1024)}, u32[]{:S(2)}) copy-start(f32[2048]{0:T(1024)} %param.17) | copy-start | bytes 24580
  285.8 354.6 %all-reduce.5.cloned.1.call-start = ((), (), s32[]{:S(2)}) async-start(), calls=%async_computation.9 | async-start | bytes 8454144 | tf_op jit(solution)/shard_map/psum | solution.py:52
  441.1 4.7 copy-start.3
  441.1 5.9 copy-start.4
  441.1 29.6 %slice-start = ((s8[8388608]{0:T(1024)(128)(4,1)}), s8[4194304]{0:T(1024)(128)(4,1)S(1)}, s32[]{:S(2)}) async-start(s8[8388608]{0:T(1024)(128)(4,1)} %bitcast.68), calls=%async_computation.10 | async-start | bytes 8388608
  447.0 23.7 %slice-start.1 = ((s8[8388608]{0:T(1024)(128)(4,1)}), s8[4194304]{0:T(1024)(128)(4,1)S(1)}, s32[]{:S(2)}) async-start(s8[8388608]{0:T(1024)(128)(4,1)} %bitcast.68), calls=%async_computation.11 | async-start | bytes 8388608
Sparse Core Ops, SparseCore 0:
  9.9 49.3 all-gather.4
  61.2 27.9 all-gather.6
  91.0 74.1 all-gather.10
  166.9 93.0 all-gather.8
  285.9 155.1 all-reduce.2
  485.2 155.0 all-reduce.4

commit v2 on v1

--- a/solution.py
+++ b/solution.py
@@ -9,6 +9,7 @@
 Q_ROWS = 512
 K_ROWS = 512
 DEC_ROWS = 1024
+DEC_PAD = 16
 
 
 rope_base = 130000.0
@@ -48,8 +49,22 @@
     return lax.all_gather(weights, "tok", axis=axis, tiled=True)
 
 
-def over_heads(partial_value):
-    return lax.psum(partial_value.astype(jnp.bfloat16), "head").astype(jnp.float32)
+def to_heads(blocks):
+    return lax.all_to_all(blocks, "head", split_axis=0, concat_axis=0, tiled=True)
+
+
+def from_heads(rows):
+    return lax.all_gather(rows, "head", axis=0, tiled=True)
+
+
+def sum_heads(partial_value):
+    return lax.psum_scatter(
+        partial_value.astype(jnp.bfloat16), "head", scatter_dimension=0, tiled=True
+    )
+
+
+def after(first, second):
+    return lax.optimization_barrier((first, second))
 
 
 def rope_tables(positions, width):
@@ -324,6 +339,10 @@
     dec_local = dec_tokens.shape[0]
     dec_total = dec_order.shape[0]
     group_width = w_qkv.shape[1]
+    head_count = lax.axis_size("head")
+    out_depth, out_width = w_out.shape
+    out_rows = to_heads(jnp.broadcast_to(w_out[None], (head_count, out_depth, out_width)))
+    out_rows = jnp.transpose(out_rows, (1, 0, 2)).reshape(out_depth, head_count * out_width)
     rows = jnp.concatenate([pre_tokens, dec_tokens], axis=0)
     normed = rms_norm(rows, attn_gain)
     projected = fold_rows(normed, whole(w_qkv, 2)).astype(jnp.bfloat16)
@@ -340,7 +359,7 @@
     offset_now = pre_offsets[0]
     pre_att = prefill_attend(pre_recv, offset_now, pre_cache)
     pre_att, out_full, gate_up_full, down_full = lax.optimization_barrier(
-        (pre_att, whole(w_out, 0), whole(w_gate_up, 2), whole(w_down, 0))
+        (pre_att, whole(out_rows, 0), whole(w_gate_up, 2), whole(w_down, 0))
     )
     own_slots = lax.dynamic_slice_in_dim(dec_order, tok_index * dec_local, dec_local)
     dec_mine = jnp.take(dec_recv, own_slots, axis=1)
@@ -364,13 +383,58 @@
     )
     pre_mixed = jnp.take(pre_ret, inverse, axis=0).reshape(span_rows, group_width)
     dec_mixed = jnp.sum(dec_ret.astype(jnp.float32), axis=0).astype(jnp.bfloat16)
-    attended = jnp.concatenate([pre_mixed, dec_mixed], axis=0)
-    resid = rows.astype(jnp.float32) + over_heads(map_rows(attended, out_full))
+    share = span_rows // head_count
+    half = share // 2
+    dec_pad = ((0, DEC_PAD - dec_local), (0, 0))
+    dec_blocks = jnp.broadcast_to(
+        jnp.pad(dec_mixed, dec_pad)[None], (head_count, DEC_PAD, group_width)
+    )
+    mixed = to_heads(
+        jnp.concatenate([pre_mixed.reshape(head_count, share, group_width), dec_blocks], axis=1)
+    )
+    attended = jnp.transpose(mixed, (1, 0, 2)).reshape(share + DEC_PAD, head_count * group_width)
+    own_rows = jnp.concatenate(
+        [
+            lax.dynamic_slice_in_dim(pre_tokens, lax.axis_index("head") * share, share),
+            jnp.pad(dec_tokens, dec_pad),
+        ],
+        axis=0,
+    )
+    resid = own_rows.astype(jnp.float32) + map_rows(attended, out_full)
     mlp_in = rms_norm(resid, mlp_gain)
-    gate_up = fold_rows(mlp_in, gate_up_full)
-    hidden = (jax.nn.silu(gate_up[0]) * gate_up[1]).astype(jnp.bfloat16)
-    final = (resid + over_heads(map_rows(hidden, down_full))).astype(jnp.bfloat16)
-    return (final[:span_rows], final[span_rows:])
+    width = mlp_in.shape[1]
+
+    def mlp_partial(inputs):
+        gate_up = fold_rows(inputs, gate_up_full)
+        hidden = (jax.nn.silu(gate_up[0]) * gate_up[1]).astype(jnp.bfloat16)
+        return map_rows(hidden, down_full).astype(jnp.bfloat16)
+
+    first_in = from_heads(mlp_in[:half])
+    first_in, second_own = after(first_in, mlp_in[half:share])
+    second_in = from_heads(second_own)
+    first_part = mlp_partial(first_in)
+    second_part = mlp_partial(jnp.concatenate([second_in, mlp_in[share:]], axis=0))
+    wide = head_count * half
+    second_part = jnp.concatenate(
+        [
+            second_part[:wide].reshape(head_count, half, width),
+            jnp.broadcast_to(second_part[wide:][None], (head_count, DEC_PAD, width)),
+        ],
+        axis=1,
+    ).reshape(head_count * (half + DEC_PAD), width)
+    first_sum = sum_heads(first_part)
+    first_sum, second_part = after(first_sum, second_part)
+    second_sum = sum_heads(second_part)
+    first_own = (resid[:half] + first_sum.astype(jnp.float32)).astype(jnp.bfloat16)
+    first_own, second_sum = after(first_own, second_sum)
+    first_out = from_heads(first_own)
+    second_own = (resid[half:] + second_sum.astype(jnp.float32)).astype(jnp.bfloat16)
+    first_out, second_own = after(first_out, second_own)
+    second_out = from_heads(second_own).reshape(head_count, half + DEC_PAD, width)
+    pre_out = jnp.concatenate(
+        [first_out.reshape(head_count, half, width), second_out[:, :half]], axis=1
+    ).reshape(span_rows, width)
+    return (pre_out, second_out[0, half : half + dec_local])
 
 
 def solution(mesh):

time: 657 us -> 657 us (level)
  blocking collectives: 0 us -> 31.9 us
  waiting for transfers between devices: 472 us -> 446 us
  Pallas kernels: 58.1 us -> 40.2 us
    psum x2 -> x0, waiting for transfers between devices: 310 us -> none  [over_heads(): lax.psum(partial_value.astype(jnp.bfloat16), 'head').astype(jnp.float32)]
    all_gather x0 -> x4, waiting for transfers between devices: none -> 167 us  [from_heads(): return lax.all_gather(rows, 'head', axis=0, tiled=True)]
    reduce_scatter x0 -> x2, waiting for transfers between devices: none -> 70.2 us  [sum_heads(): lax.psum_scatter(partial_value.astype(jnp.bfloat16), 'head', scatter_dime...]
    all_to_all x0 -> x1, blocking collectives: none -> 31.9 us  [to_heads(): lax.all_to_all(blocks, 'head', split_axis=0, concat_axis=0, tiled=True)]
    all_to_all x0 -> x1, waiting for transfers between devices: none -> 23 us  [to_heads(): lax.all_to_all(blocks, 'head', split_axis=0, concat_axis=0, tiled=True)]
    pallas_call x1, Pallas kernels: 52.6 us -> 35.6 us  [prefill_attend(): pl.pallas_call(prefill_kernel, out_shape=jax.ShapeDtypeStruct((span, widt...]
    all_gather x4, waiting for transfers between devices: 110 us -> 125 us  [whole(): return lax.all_gather(weights, 'tok', axis=axis, tiled=True)]
    all_to_all x1, waiting for transfers between devices: 33.5 us -> 44.3 us  [on_device(): lax.all_to_all(pre_send, 'tok', split_axis=1, concat_axis=1, tiled=True)]
  transfers between devices with their start and end apart: 10 -> 15, of which waited for: 6 -> 12; matrix products, arithmetic and copies ran while one was open for 4% -> 12% of each run, Pallas kernels for 9% -> 6%
where the time goes in v2:
time: 657 us; the launch traced here: 656 us
  waiting for transfers between devices  446 us (68%)
  matrix products  59.8 us (9%)
  Pallas kernels  40.2 us (6%)
  blocking collectives  31.9 us (5%)
  local copies, waits for them, and re-layouts  23.7 us (4%)
  starting transfers between devices  20.2 us (3%)
  other arithmetic  18.1 us (3%)
  between operations  15.2 us (2%)
    all_gather x4, waiting for transfers between devices, from_heads(): return lax.all_gather(rows, 'head', axis=0, tiled=True)  167 us
    all_gather x4, waiting for transfers between devices, whole(): return lax.all_gather(weights, 'tok', axis=axis, tiled=True)  125 us
    reduce_scatter x2, waiting for transfers between devices, sum_heads(): lax.psum_scatter(partial_value.astype(jnp.bfloat16), 'head', scatter_dime...  70.2 us
    all_to_all x1, waiting for transfers between devices, on_device(): lax.all_to_all(pre_send, 'tok', split_axis=1, concat_axis=1, tiled=True)  44.3 us
    dot_general x3, matrix products, fold_rows(): jnp.einsum('td,kcd->ktc', inputs, weights, preferred_element_type=jnp.flo...  35.8 us
    pallas_call x1, Pallas kernels, prefill_attend(): pl.pallas_call(prefill_kernel, out_shape=jax.ShapeDtypeStruct((span, widt...  35.6 us
    all_to_all x1, blocking collectives, to_heads(): lax.all_to_all(blocks, 'head', split_axis=0, concat_axis=0, tiled=True)  31.9 us
    dot_general x3, matrix products, map_rows(): jnp.einsum('tc,dc->td', inputs, weights, preferred_element_type=jnp.float32)  23.9 us
  transfers between devices with their start and end apart: 15, of which 12 were waited for; matrix products, arithmetic and copies ran while one was open for 12% of the time, Pallas kernels for 6%

profile of v2, /device:TPU:0, one launch (start us, length us, event | category | flops | bytes accessed | tf_op | source)
XLA Modules:
  0.0 655.5 jit_solution(9367344222239955749)
XLA Ops:
  9.9 31.9 %all_to_all.30 = bf16[4,256,512]{1,2,0:T(8,128)(2,1)} all-to-all(bf16[4,256,512]{1,2,0:T(8,128)(2,1)S(1)} %broadcast_in_dim.127), channel_id=1, replica_groups=mesh['tok'=8,'head'=4] {'head'}, dimensions={0} | all-to-all | bytes 2097152 | tf_op jit(solution)/shard_map/all_to_all | solution.py:53
  45.6 13.7 %all-gather.9.cloned.1.call-done = bf16[3,512,2048]{2,1,0:T(8,128)(2,1)} async-done(((bf16[3,512,256]{2,1,0:T(8,128)(2,1)}), bf16[3,512,2048]{2,1,0:T(8,128)(2,1)}) %all-gather.9.cloned.1.call-update) | async-done | bytes 6291472 | tf_op jit(solution)/shard_map/all_gather | solution.py:49
  59.3 10.4 %fusion.11 = bf16[3,1026,512]{2,1,0:T(8,128)(2,1)S(1)} fusion(bf16[3,512,2048]{2,1,0:T(8,128)(2,1)} %all-gather.9.cloned.1.call-done, f32[2048]{0:T(1024)S(1)} %copy-done.7, f32[1026]{0:T(1024)S(1)} %add_rsqrt_fusion, bf16[2,2048]{1,0:T(2,128)(2,1)S(1)} %copy-done.4, bf16[1024,2048]{1,0:T(8,128)(2,1)} %param.14), kind=kOutput, calls=%fused_computation.24 | convolution fusion | flops 6471318528 | bytes 13658120 | tf_op jit(solution)/shard_map/td,kcd->ktc/dot_general | solution.py:41
  80.3 4.6 all-to-all-start
  88.4 7.1 %copy-done = bf16[2,2,4096,512]{3,2,1,0:T(8,128)(2,1)S(1)} copy-done((bf16[2,2,4096,512]{3,2,1,0:T(8,128)(2,1)S(1)}, bf16[2,2,4096,512]{3,2,1,0:T(8,128)(2,1)}, u32[]{:S(2)}) %copy-start) | copy-done | bytes 16777240
  95.5 4.6 decode_attend.1
  100.9 44.3 %all-to-all-done = bf16[3,8,128,512]{3,2,0,1:T(8,128)(2,1)} async-done(((bf16[3,8,128,512]{3,2,0,1:T(8,128)(2,1)}), bf16[3,8,128,512]{3,2,0,1:T(8,128)(2,1)}, u32[]{:S(2)}, u32[]{:S(2)}) %all-to-all-start) | async-done | bytes 3145760 | tf_op jit(solution)/shard_map/all_to_all | solution.py:354
  151.8 35.6 %prefill_attend.1 = bf16[1024,512]{1,0:T(8,128)(2,1)} custom-call(s32[1]{0:T(128)} %copy.58.limit_ref, bf16[3,1024,512]{2,1,0:T(8,128)(2,1)S(1)} %bitcast.95, bf16[3,1024,512]{2,1,0:T(8,128)(2,1)S(1)} %bitcast.96, bf16[3,1024,512]{2,1,0:T(8,128)(2,1)S(1)} %bitcast.97, f32[1024,128]{1,0:T(8,128)S(1)} %copy.45.cos_ref, f32[1024,128]{1,0:T(8,128)S(1)} %copy.46.sin_ref, ...), custom_call_target="tpu_custom_call" | custom-call | flops 25769803776 | bytes 8388608 | tf_op jit(solution)/shard_map/prefill_attend/pallas_call | solution.py:197
  187.4 16.7 %all-gather.11.cloned.1.call-done = bf16[2048,2048]{0,1:T(8,128)(2,1)} async-done(((bf16[256,2048]{0,1:T(8,128)(2,1)}), bf16[2048,2048]{0,1:T(8,128)(2,1)}) %all-gather.11.cloned.1.call-update) | async-done | bytes 8388624 | tf_op jit(solution)/shard_map/all_gather | solution.py:49
  204.0 94.9 %all-gather.13.cloned.1.call-done = bf16[2,2048,2048]{2,1,0:T(8,128)(2,1)} async-done(((bf16[2,2048,256]{2,1,0:T(8,128)(2,1)}), bf16[2,2048,2048]{2,1,0:T(8,128)(2,1)}) %all-gather.13.cloned.1.call-update) | async-done | bytes 16777232 | tf_op jit(solution)/shard_map/all_gather | solution.py:49
  302.9 14.9 %all-to-all-done.2 = bf16[8,128,512]{2,1,0:T(8,128)(2,1)S(1)} async-done(((bf16[8,128,512]{2,1,0:T(8,128)(2,1)}), bf16[8,128,512]{2,1,0:T(8,128)(2,1)S(1)}, u32[]{:S(2)}, u32[]{:S(2)}) %all-to-all-start.2) | async-done | bytes 1048608 | tf_op jit(solution)/shard_map/all_to_all | solution.py:377
  319.7 4.6 all-to-all-start.5
  325.6 23.0 %all-to-all-done.5 = bf16[4,272,512]{2,1,0:T(8,128)(2,1)S(1)} async-done(((bf16[4,272,512]{2,1,0:T(8,128)(2,1)}), bf16[4,272,512]{2,1,0:T(8,128)(2,1)S(1)}, u32[]{:S(2)}, u32[]{:S(2)}) %all-to-all-start.5) | async-done | bytes 1114144 | tf_op jit(solution)/shard_map/all_to_all | solution.py:53
  348.7 6.1 multiply_reduce_fusion
  356.2 46.3 %all-gather.17.cloned.1.call-done = bf16[512,2048]{1,0:T(8,128)(2,1)} async-done(((bf16[128,2048]{1,0:T(8,128)(2,1)}), bf16[512,2048]{1,0:T(8,128)(2,1)}) %all-gather.17.cloned.1.call-update) | async-done | bytes 2097168 | tf_op jit(solution)/shard_map/all_gather | solution.py:57
  402.8 12.7 %convolution_bitcast_fusion.1 = f32[2,512,2048]{1,2,0:T(8,128)S(1)} fusion(bf16[2,2048,2048]{2,1,0:T(8,128)(2,1)} %all-gather.13.cloned.1.call-done, bf16[512,2048]{1,0:T(8,128)(2,1)} %all-gather.17.cloned.1.call-done), kind=kOutput, calls=%fused_computation.14 | convolution fusion | flops 8589934592 | bytes 27262976 | tf_op jit(solution)/shard_map/td,kcd->ktc/dot_general | solution.py:41
  415.6 9.4 %convolution_convert_fusion.2 = bf16[512,2048]{1,0:T(8,128)(2,1)} fusion(bf16[2048,2048]{1,0:T(8,128)(2,1)} %all-gather.15.cloned.1.call-done, f32[2,512,2048]{1,2,0:T(8,128)S(1)} %convolution_bitcast_fusion.1), kind=kOutput, calls=%fused_computation.27 | convolution fusion | flops 4302307328 | bytes 18874368 | tf_op jit(solution)/shard_map/tc,dc->td/dot_general | solution.py:45
  425.1 24.1 %all-gather.19.cloned.1.call-done = bf16[512,2048]{1,0:T(8,128)(2,1)} async-done(((bf16[128,2048]{1,0:T(8,128)(2,1)}), bf16[512,2048]{1,0:T(8,128)(2,1)}) %all-gather.19.cloned.1.call-update) | async-done | bytes 2097168 | tf_op jit(solution)/shard_map/all_gather | solution.py:57
  449.2 12.7 %convolution_bitcast_fusion = f32[2,528,2048]{2,1,0:T(8,128)S(1)} fusion(bf16[2,2048,2048]{2,1,0:T(8,128)(2,1)} %all-gather.13.cloned.1.call-done, bf16[16,2048]{1,0:T(8,128)(2,1)S(1)} %slice.110, bf16[512,2048]{1,0:T(8,128)(2,1)} %all-gather.19.cloned.1.call-done), kind=kOutput, calls=%fused_computation.9 | convolution fusion | flops 8862695424 | bytes 27590656 | tf_op jit(solution)/shard_map/td,kcd->ktc/dot_general | solution.py:41
  462.0 8.4 %convolution_convert_fusion.1 = bf16[528,2048]{1,0:T(8,128)(2,1)S(1)} fusion(bf16[2048,2048]{1,0:T(8,128)(2,1)} %all-gather.15.cloned.1.call-done, f32[2,528,2048]{2,1,0:T(8,128)S(1)} %convolution_bitcast_fusion), kind=kOutput, calls=%fused_computation.26 | convolution fusion | flops 4436754432 | bytes 19202048 | tf_op jit(solution)/shard_map/tc,dc->td/dot_general | solution.py:45
  472.3 21.9 %reduce-scatter.3.cloned.1.call-done = bf16[128,2048]{1,0:T(8,128)(2,1)} async-done(((bf16[512,2048]{1,0:T(8,128)(2,1)}), bf16[128,2048]{1,0:T(8,128)(2,1)}) %reduce-scatter.3.cloned.1.call-update) | async-done | bytes 524304 | tf_op jit(solution)/shard_map/reduce_scatter | solution.py:61
  496.2 48.3 %reduce-scatter.5.cloned.1.call-done = bf16[144,2048]{1,0:T(8,128)(2,1)} async-done(((bf16[576,2048]{1,0:T(8,128)(2,1)}), bf16[144,2048]{1,0:T(8,128)(2,1)}) %reduce-scatter.5.cloned.1.call-update) | async-done | bytes 589840 | tf_op jit(solution)/shard_map/reduce_scatter | solution.py:61
  546.6 45.0 %all-gather.21.cloned.1.call-done = bf16[512,2048]{1,0:T(8,128)(2,1)} async-done(((bf16[128,2048]{1,0:T(8,128)(2,1)}), bf16[512,2048]{1,0:T(8,128)(2,1)}) %all-gather.21.cloned.1.call-update) | async-done | bytes 2097168 | tf_op jit(solution)/shard_map/all_gather | solution.py:57
  591.6 51.3 %all-gather.23.cloned.1.call-done = bf16[576,2048]{1,0:T(8,128)(2,1)} async-done(((bf16[144,2048]{1,0:T(8,128)(2,1)}), bf16[576,2048]{1,0:T(8,128)(2,1)}) %all-gather.23.cloned.1.call-update) | async-done | bytes 2359312 | tf_op jit(solution)/shard_map/all_gather | solution.py:57
  (115 shorter events, 47.9 us)
Async XLA Ops:
  7.2 52.1 %all-gather.9.cloned.1.call-start = ((), (), s32[]{:S(2)}) async-start(), calls=%async_computation.8 | async-start | bytes 7077888 | tf_op jit(solution)/shard_map/all_gather | solution.py:49
  7.9 34.5 %copy-start.8 = (s32[8]{0:T(128)S(1)}, s32[8]{0:T(128)}, u32[]{:S(2)}) copy-start(s32[8]{0:T(128)} %param.24) | copy-start | bytes 100
  7.9 34.6 %copy-start.4 = (bf16[2,2048]{1,0:T(2,128)(2,1)S(1)}, bf16[2,2048]{1,0:T(2,128)(2,1)}, u32[]{:S(2)}) copy-start(bf16[2,2048]{1,0:T(2,128)(2,1)} %param.15) | copy-start | bytes 24580
  7.9 179.5 %all-gather.15.cloned.1.call-start = ((), (), s32[]{:S(2)}) async-start(), calls=%async_computation.11 | async-start | bytes 9437184 | tf_op jit(solution)/shard_map/all_gather | solution.py:49
  8.7 195.4 %all-gather.11.cloned.1.call-start = ((), (), s32[]{:S(2)}) async-start(), calls=%async_computation.9 | async-start | bytes 9437184 | tf_op jit(solution)/shard_map/all_gather | solution.py:49
  41.8 17.4 %copy-start.7 = (f32[2048]{0:T(1024)S(1)}, f32[2048]{0:T(1024)}, u32[]{:S(2)}) copy-start(f32[2048]{0:T(1024)} %param.16) | copy-start | bytes 24580
  41.9 257.1 %all-gather.13.cloned.1.call-start = ((), (), s32[]{:S(2)}) async-start(), calls=%async_computation.10 | async-start | bytes 18874368 | tf_op jit(solution)/shard_map/all_gather | solution.py:49
  70.6 9.7 %all-to-all-start.3 = ((bf16[3,8,2,512]{3,2,0,1:T(2,128)(2,1)}), bf16[3,8,2,512]{3,2,0,1:T(2,128)(2,1)S(1)}, u32[]{:S(2)}, u32[]{:S(2)}) async-start(bf16[3,8,2,512]{3,2,0,1:T(2,128)(2,1)} %broadcast_in_dim.133), calls=%async_computation.3 | async-start | bytes 98304 | tf_op jit(solution)/shard_map/all_to_all | solution.py:355
  80.3 4.8 copy-start.1
  80.3 6.6 %copy-start.6 = (s32[16]{0:T(128)S(1)}, s32[16]{0:T(128)}, u32[]{:S(2)}) copy-start(s32[16]{0:T(128)} %param.25) | copy-start | bytes 196
  80.3 64.9 %all-to-all-start = ((bf16[3,8,128,512]{3,2,0,1:T(8,128)(2,1)}), bf16[3,8,128,512]{3,2,0,1:T(8,128)(2,1)}, u32[]{:S(2)}, u32[]{:S(2)}) async-start(bf16[3,8,128,512]{3,2,0,1:T(8,128)(2,1)} %select_bitcast_fusion), calls=%async_computation | async-start | bytes 6291456 | tf_op jit(solution)/shard_map/all_to_all | solution.py:354
  88.4 7.2 %copy-start = (bf16[2,2,4096,512]{3,2,1,0:T(8,128)(2,1)S(1)}, bf16[2,2,4096,512]{3,2,1,0:T(8,128)(2,1)}, u32[]{:S(2)}) copy-start(bf16[2,2,4096,512]{3,2,1,0:T(8,128)(2,1)} %cache_ref.3) | copy-start | bytes 50331652
  145.2 153.8 %all-to-all-start.4 = ((bf16[8,2,512]{2,1,0:T(2,128)(2,1)}), bf16[8,2,512]{2,1,0:T(2,128)(2,1)S(1)}, u32[]{:S(2)}, u32[]{:S(2)}) async-start(bf16[8,2,512]{2,1,0:T(2,128)(2,1)} %reshape.216), calls=%async_computation.4 | async-start | bytes 32768 | tf_op jit(solution)/shard_map/all_to_all | solution.py:378
  148.7 3.1 copy-start.2
  298.9 18.9 %all-to-all-start.2 = ((bf16[8,128,512]{2,1,0:T(8,128)(2,1)}), bf16[8,128,512]{2,1,0:T(8,128)(2,1)S(1)}, u32[]{:S(2)}, u32[]{:S(2)}) async-start(bf16[8,128,512]{2,1,0:T(8,128)(2,1)} %bitcast.11), calls=%async_computation.2 | async-start | bytes 2097152 | tf_op jit(solution)/shard_map/all_to_all | solution.py:377
  319.7 28.9 %all-to-all-start.5 = ((bf16[4,272,512]{2,1,0:T(8,128)(2,1)}), bf16[4,272,512]{2,1,0:T(8,128)(2,1)S(1)}, u32[]{:S(2)}, u32[]{:S(2)}) async-start(bf16[4,272,512]{2,1,0:T(8,128)(2,1)} %pad_maximum_fusion.4), calls=%async_computation.5 | async-start | bytes 2228224 | tf_op jit(solution)/shard_map/all_to_all | solution.py:53
  324.3 78.2 %all-gather.17.cloned.1.call-start = ((), (), s32[]{:S(2)}) async-start(), calls=%async_computation.12 | async-start | bytes 2621440 | tf_op jit(solution)/shard_map/all_gather | solution.py:57
  348.7 6.1 copy-start.5
  356.2 93.0 %all-gather.19.cloned.1.call-start = ((), (), s32[]{:S(2)}) async-start(), calls=%async_computation.14 | async-start | bytes 2621440 | tf_op jit(solution)/shard_map/all_gather | solution.py:57
  402.6 91.5 %reduce-scatter.3.cloned.1.call-start = ((), (), s32[]{:S(2)}) async-start(), calls=%async_computation.13 | async-start | bytes 2621440 | tf_op jit(solution)/shard_map/reduce_scatter | solution.py:61
  425.1 119.4 %reduce-scatter.5.cloned.1.call-start = ((), (), s32[]{:S(2)}) async-start(), calls=%async_computation.15 | async-start | bytes 2949120 | tf_op jit(solution)/shard_map/reduce_scatter | solution.py:61
  494.2 97.5 %all-gather.21.cloned.1.call-start = ((), (), s32[]{:S(2)}) async-start(), calls=%async_computation.16 | async-start | bytes 2621440 | tf_op jit(solution)/shard_map/all_gather | solution.py:57
  544.5 98.4 %all-gather.23.cloned.1.call-start = ((), (), s32[]{:S(2)}) async-start(), calls=%async_computation.17 | async-start | bytes 2949120 | tf_op jit(solution)/shard_map/all_gather | solution.py:57
  591.6 54.5 %copy-start.3 = (bf16[512,2048]{1,0:T(8,128)(2,1)S(1)}, bf16[512,2048]{1,0:T(8,128)(2,1)}, u32[]{:S(2)}) copy-start(bf16[512,2048]{1,0:T(8,128)(2,1)} %all-gather.21.cloned.1.call-done) | copy-start | bytes 6291460
Sparse Core Ops, SparseCore 0:
  9.9 49.3 all-gather.8
  61.2 77.1 all-gather.14
  140.2 63.7 all-gather.10
  205.8 93.1 all-gather.12
  356.3 46.1 all-gather.16
  404.6 44.6 all-gather.18
  451.5 42.5 reduce-scatter.2
  497.1 47.3 reduce-scatter.4
  546.2 45.4 all-gather.20
  593.7 49.1 all-gather.22

commit v3 on v2

--- a/solution.py
+++ b/solution.py
@@ -358,9 +358,7 @@
     dec_recv = dec_recv.reshape(3, dec_total, group_width)
     offset_now = pre_offsets[0]
     pre_att = prefill_attend(pre_recv, offset_now, pre_cache)
-    pre_att, out_full, gate_up_full, down_full = lax.optimization_barrier(
-        (pre_att, whole(out_rows, 0), whole(w_gate_up, 2), whole(w_down, 0))
-    )
+    out_full = whole(out_rows, 0)
     own_slots = lax.dynamic_slice_in_dim(dec_order, tok_index * dec_local, dec_local)
     dec_mine = jnp.take(dec_recv, own_slots, axis=1)
     dec_att = decode_attend(dec_mine, dec_lengths, dec_cache)
@@ -403,6 +401,9 @@
     resid = own_rows.astype(jnp.float32) + map_rows(attended, out_full)
     mlp_in = rms_norm(resid, mlp_gain)
     width = mlp_in.shape[1]
+    mlp_in, gate_up_full, down_full = lax.optimization_barrier(
+        (mlp_in, whole(w_gate_up, 2), whole(w_down, 0))
+    )
 
     def mlp_partial(inputs):
         gate_up = fold_rows(inputs, gate_up_full)

time: 657 us -> 604 us (0.919)
  waiting for transfers between devices: 446 us -> 377 us
  starting transfers between devices: 20.2 us -> 36.7 us
    all_gather x4, waiting for transfers between devices: 125 us -> 51.4 us  [whole(): return lax.all_gather(weights, 'tok', axis=axis, tiled=True)]
    all_to_all x1, starting transfers between devices: 3.56 us -> 20.1 us  [on_device(): lax.all_to_all(pre_back, 'tok', split_axis=0, concat_axis=0, tiled=True)]
  transfers between devices with their start and end apart: 15 -> 15, of which waited for: 12 -> 11; matrix products, arithmetic and copies ran while one was open for 12% -> 15% of each run, Pallas kernels for 6% -> 7%
where the time goes in v3:
time: 604 us; the launch traced here: 603 us
  waiting for transfers between devices  377 us (62%)
  matrix products  60.3 us (10%)
  Pallas kernels  39.3 us (7%)
  starting transfers between devices  36.7 us (6%)
  blocking collectives  31.9 us (5%)
  local copies, waits for them, and re-layouts  24.8 us (4%)
  other arithmetic  18.1 us (3%)
  between operations  15.2 us (3%)
    all_gather x4, waiting for transfers between devices, from_heads(): return lax.all_gather(rows, 'head', axis=0, tiled=True)  167 us
    reduce_scatter x2, waiting for transfers between devices, sum_heads(): lax.psum_scatter(partial_value.astype(jnp.bfloat16), 'head', scatter_dime...  70.2 us
    all_gather x4, waiting for transfers between devices, whole(): return lax.all_gather(weights, 'tok', axis=axis, tiled=True)  51.4 us
    all_to_all x1, waiting for transfers between devices, on_device(): lax.all_to_all(pre_send, 'tok', split_axis=1, concat_axis=1, tiled=True)  45.1 us
    dot_general x3, matrix products, fold_rows(): jnp.einsum('td,kcd->ktc', inputs, weights, preferred_element_type=jnp.flo...  35.8 us
    pallas_call x1, Pallas kernels, prefill_attend(): pl.pallas_call(prefill_kernel, out_shape=jax.ShapeDtypeStruct((span, widt...  35.6 us
    all_to_all x1, blocking collectives, to_heads(): lax.all_to_all(blocks, 'head', split_axis=0, concat_axis=0, tiled=True)  31.9 us
    dot_general x3, matrix products, map_rows(): jnp.einsum('tc,dc->td', inputs, weights, preferred_element_type=jnp.float32)  24.3 us
  transfers between devices with their start and end apart: 15, of which 11 were waited for; matrix products, arithmetic and copies ran while one was open for 15% of the time, Pallas kernels for 7%

profile of v3, /device:TPU:0, one launch (start us, length us, event | category | flops | bytes accessed | tf_op | source)
XLA Modules:
  0.0 603.3 jit_solution(7941545878923222203)
XLA Ops:
  9.1 31.9 %all_to_all.30 = bf16[4,256,512]{1,2,0:T(8,128)(2,1)} all-to-all(bf16[4,256,512]{1,2,0:T(8,128)(2,1)S(1)} %broadcast_in_dim.138), channel_id=1, replica_groups=mesh['tok'=8,'head'=4] {'head'}, dimensions={0} | all-to-all | bytes 2097152 | tf_op jit(solution)/shard_map/all_to_all | solution.py:53
  45.6 13.7 %all-gather.9.cloned.1.call-done = bf16[3,512,2048]{2,1,0:T(8,128)(2,1)} async-done(((bf16[3,512,256]{2,1,0:T(8,128)(2,1)}), bf16[3,512,2048]{2,1,0:T(8,128)(2,1)}) %all-gather.9.cloned.1.call-update) | async-done | bytes 6291472 | tf_op jit(solution)/shard_map/all_gather | solution.py:49
  59.3 10.4 %fusion.11 = bf16[3,1026,512]{2,1,0:T(8,128)(2,1)S(1)} fusion(bf16[3,512,2048]{2,1,0:T(8,128)(2,1)} %all-gather.9.cloned.1.call-done, f32[2048]{0:T(1024)S(1)} %copy-done.7, f32[1026]{0:T(1024)S(1)} %add_rsqrt_fusion, bf16[2,2048]{1,0:T(2,128)(2,1)S(1)} %copy-done.4, bf16[1024,2048]{1,0:T(8,128)(2,1)} %param.14), kind=kOutput, calls=%fused_computation.24 | convolution fusion | flops 6471318528 | bytes 13658120 | tf_op jit(solution)/shard_map/td,kcd->ktc/dot_general | solution.py:41
  76.3 3.9 select_bitcast_fusion
  80.3 4.6 all-to-all-start
  88.4 7.1 %copy-done = bf16[2,2,4096,512]{3,2,1,0:T(8,128)(2,1)S(1)} copy-done((bf16[2,2,4096,512]{3,2,1,0:T(8,128)(2,1)S(1)}, bf16[2,2,4096,512]{3,2,1,0:T(8,128)(2,1)}, u32[]{:S(2)}) %copy-start) | copy-done | bytes 16777240
  100.0 45.1 %all-to-all-done = bf16[3,8,128,512]{3,2,0,1:T(8,128)(2,1)} async-done(((bf16[3,8,128,512]{3,2,0,1:T(8,128)(2,1)}), bf16[3,8,128,512]{3,2,0,1:T(8,128)(2,1)}, u32[]{:S(2)}, u32[]{:S(2)}) %all-to-all-start) | async-done | bytes 3145760 | tf_op jit(solution)/shard_map/all_to_all | solution.py:354
  151.8 35.6 %prefill_attend.1 = bf16[1024,512]{1,0:T(8,128)(2,1)} custom-call(s32[1]{0:T(128)} %copy.58.limit_ref, bf16[3,1024,512]{2,1,0:T(8,128)(2,1)S(1)} %bitcast.95, bf16[3,1024,512]{2,1,0:T(8,128)(2,1)S(1)} %bitcast.96, bf16[3,1024,512]{2,1,0:T(8,128)(2,1)S(1)} %bitcast.97, f32[1024,128]{1,0:T(8,128)S(1)} %copy.45.cos_ref, f32[1024,128]{1,0:T(8,128)S(1)} %copy.46.sin_ref, ...), custom_call_target="tpu_custom_call" | custom-call | flops 25769803776 | bytes 8388608 | tf_op jit(solution)/shard_map/prefill_attend/pallas_call | solution.py:197
  187.4 20.1 %all-to-all-start.1 = ((bf16[8,128,512]{2,1,0:T(8,128)(2,1)}), bf16[8,128,512]{2,1,0:T(8,128)(2,1)S(1)}, u32[]{:S(2)}, u32[]{:S(2)}) async-start(bf16[8,128,512]{2,1,0:T(8,128)(2,1)} %bitcast.9), calls=%async_computation.1 | async-start | bytes 2097152 | tf_op jit(solution)/shard_map/all_to_all | solution.py:375
  207.9 19.7 %all-to-all-done.1 = bf16[8,128,512]{2,1,0:T(8,128)(2,1)S(1)} async-done(((bf16[8,128,512]{2,1,0:T(8,128)(2,1)}), bf16[8,128,512]{2,1,0:T(8,128)(2,1)S(1)}, u32[]{:S(2)}, u32[]{:S(2)}) %all-to-all-start.1) | async-done | bytes 1048608 | tf_op jit(solution)/shard_map/all_to_all | solution.py:375
  229.5 4.6 all-to-all-start.4
  236.4 21.8 %all-to-all-done.4 = bf16[4,272,512]{2,1,0:T(8,128)(2,1)S(1)} async-done(((bf16[4,272,512]{2,1,0:T(8,128)(2,1)}), bf16[4,272,512]{2,1,0:T(8,128)(2,1)S(1)}, u32[]{:S(2)}, u32[]{:S(2)}) %all-to-all-start.4) | async-done | bytes 1114144 | tf_op jit(solution)/shard_map/all_to_all | solution.py:53
  258.5 6.5 %multiply_reduce_fusion = (f32[272]{0:T(512)S(1)}, f32[272,2048]{1,0:T(8,128)S(1)}) fusion(bf16[272,2048]{1,0:T(8,128)(2,1)S(1)} %bitcast.110, bf16[2048,2048]{0,1:T(8,128)(2,1)} %all-gather.11.cloned.1.call-done, bf16[2,2048]{1,0:T(2,128)(2,1)S(1)} %copy-done.4, bf16[256,2048]{1,0:T(8,128)(2,1)} %constant_dynamic-slice_fusion), kind=kOutput, calls=%fused_computation.32 | convolution fusion | flops 2286714624 | bytes 12788800 | tf_op jit(solution)/shard_map/tc,dc->td/dot_general | solution.py:45
  265.3 37.6 %all-gather.13.cloned.1.call-done = bf16[2,2048,2048]{2,1,0:T(8,128)(2,1)} async-done(((bf16[2,2048,256]{2,1,0:T(8,128)(2,1)}), bf16[2,2048,2048]{2,1,0:T(8,128)(2,1)}) %all-gather.13.cloned.1.call-update) | async-done | bytes 16777232 | tf_op jit(solution)/shard_map/all_gather | solution.py:49
  304.0 46.2 %all-gather.17.cloned.1.call-done = bf16[512,2048]{1,0:T(8,128)(2,1)} async-done(((bf16[128,2048]{1,0:T(8,128)(2,1)}), bf16[512,2048]{1,0:T(8,128)(2,1)}) %all-gather.17.cloned.1.call-update) | async-done | bytes 2097168 | tf_op jit(solution)/shard_map/all_gather | solution.py:57
  350.6 12.7 %convolution_bitcast_fusion.1 = f32[2,512,2048]{1,2,0:T(8,128)S(1)} fusion(bf16[2,2048,2048]{2,1,0:T(8,128)(2,1)} %all-gather.13.cloned.1.call-done, bf16[512,2048]{1,0:T(8,128)(2,1)} %all-gather.17.cloned.1.call-done), kind=kOutput, calls=%fused_computation.14 | convolution fusion | flops 8589934592 | bytes 27262976 | tf_op jit(solution)/shard_map/td,kcd->ktc/dot_general | solution.py:41
  363.3 9.4 %convolution_convert_fusion.2 = bf16[512,2048]{1,0:T(8,128)(2,1)} fusion(bf16[2048,2048]{1,0:T(8,128)(2,1)} %all-gather.15.cloned.1.call-done, f32[2,512,2048]{1,2,0:T(8,128)S(1)} %convolution_bitcast_fusion.1), kind=kOutput, calls=%fused_computation.27 | convolution fusion | flops 4302307328 | bytes 18874368 | tf_op jit(solution)/shard_map/tc,dc->td/dot_general | solution.py:45
  372.8 24.1 %all-gather.19.cloned.1.call-done = bf16[512,2048]{1,0:T(8,128)(2,1)} async-done(((bf16[128,2048]{1,0:T(8,128)(2,1)}), bf16[512,2048]{1,0:T(8,128)(2,1)}) %all-gather.19.cloned.1.call-update) | async-done | bytes 2097168 | tf_op jit(solution)/shard_map/all_gather | solution.py:57
  397.0 12.7 %convolution_bitcast_fusion = f32[2,528,2048]{2,1,0:T(8,128)S(1)} fusion(bf16[2,2048,2048]{2,1,0:T(8,128)(2,1)} %all-gather.13.cloned.1.call-done, bf16[16,2048]{1,0:T(8,128)(2,1)S(1)} %slice.82, bf16[512,2048]{1,0:T(8,128)(2,1)} %all-gather.19.cloned.1.call-done), kind=kOutput, calls=%fused_computation.9 | convolution fusion | flops 8862695424 | bytes 27590656 | tf_op jit(solution)/shard_map/td,kcd->ktc/dot_general | solution.py:41
  409.7 8.4 %convolution_convert_fusion.1 = bf16[528,2048]{1,0:T(8,128)(2,1)S(1)} fusion(bf16[2048,2048]{1,0:T(8,128)(2,1)} %all-gather.15.cloned.1.call-done, f32[2,528,2048]{2,1,0:T(8,128)S(1)} %convolution_bitcast_fusion), kind=kOutput, calls=%fused_computation.26 | convolution fusion | flops 4436754432 | bytes 19202048 | tf_op jit(solution)/shard_map/tc,dc->td/dot_general | solution.py:45
  420.0 21.9 %reduce-scatter.3.cloned.1.call-done = bf16[128,2048]{1,0:T(8,128)(2,1)} async-done(((bf16[512,2048]{1,0:T(8,128)(2,1)}), bf16[128,2048]{1,0:T(8,128)(2,1)}) %reduce-scatter.3.cloned.1.call-update) | async-done | bytes 524304 | tf_op jit(solution)/shard_map/reduce_scatter | solution.py:61
  443.9 48.4 %reduce-scatter.5.cloned.1.call-done = bf16[144,2048]{1,0:T(8,128)(2,1)} async-done(((bf16[576,2048]{1,0:T(8,128)(2,1)}), bf16[144,2048]{1,0:T(8,128)(2,1)}) %reduce-scatter.5.cloned.1.call-update) | async-done | bytes 589840 | tf_op jit(solution)/shard_map/reduce_scatter | solution.py:61
  494.3 45.0 %all-gather.21.cloned.1.call-done = bf16[512,2048]{1,0:T(8,128)(2,1)} async-done(((bf16[128,2048]{1,0:T(8,128)(2,1)}), bf16[512,2048]{1,0:T(8,128)(2,1)}) %all-gather.21.cloned.1.call-update) | async-done | bytes 2097168 | tf_op jit(solution)/shard_map/all_gather | solution.py:57
  539.4 51.3 %all-gather.23.cloned.1.call-done = bf16[576,2048]{1,0:T(8,128)(2,1)} async-done(((bf16[144,2048]{1,0:T(8,128)(2,1)}), bf16[576,2048]{1,0:T(8,128)(2,1)}) %all-gather.23.cloned.1.call-update) | async-done | bytes 2359312 | tf_op jit(solution)/shard_map/all_gather | solution.py:57
  (115 shorter events, 45.2 us)
Async XLA Ops:
  7.2 52.1 %all-gather.9.cloned.1.call-start = ((), (), s32[]{:S(2)}) async-start(), calls=%async_computation.8 | async-start | bytes 7077888 | tf_op jit(solution)/shard_map/all_gather | solution.py:49
  7.9 34.5 %copy-start.8 = (s32[8]{0:T(128)S(1)}, s32[8]{0:T(128)}, u32[]{:S(2)}) copy-start(s32[8]{0:T(128)} %param.24) | copy-start | bytes 100
  7.9 34.6 %copy-start.4 = (bf16[2,2048]{1,0:T(2,128)(2,1)S(1)}, bf16[2,2048]{1,0:T(2,128)(2,1)}, u32[]{:S(2)}) copy-start(bf16[2,2048]{1,0:T(2,128)(2,1)} %param.15) | copy-start | bytes 24580
  7.9 250.5 %all-gather.11.cloned.1.call-start = ((), (), s32[]{:S(2)}) async-start(), calls=%async_computation.9 | async-start | bytes 9437184 | tf_op jit(solution)/shard_map/all_gather | solution.py:49
  41.1 18.2 %copy-start.7 = (f32[2048]{0:T(1024)S(1)}, f32[2048]{0:T(1024)}, u32[]{:S(2)}) copy-start(f32[2048]{0:T(1024)} %param.16) | copy-start | bytes 24580
  41.1 224.1 %all-gather.15.cloned.1.call-start = ((), (), s32[]{:S(2)}) async-start(), calls=%async_computation.11 | async-start | bytes 9437184 | tf_op jit(solution)/shard_map/all_gather | solution.py:49
  41.8 261.0 %all-gather.13.cloned.1.call-start = ((), (), s32[]{:S(2)}) async-start(), calls=%async_computation.10 | async-start | bytes 18874368 | tf_op jit(solution)/shard_map/all_gather | solution.py:49
  70.6 9.7 %all-to-all-start.2 = ((bf16[3,8,2,512]{3,2,0,1:T(2,128)(2,1)}), bf16[3,8,2,512]{3,2,0,1:T(2,128)(2,1)S(1)}, u32[]{:S(2)}, u32[]{:S(2)}) async-start(bf16[3,8,2,512]{3,2,0,1:T(2,128)(2,1)} %broadcast_in_dim.132), calls=%async_computation.2 | async-start | bytes 98304 | tf_op jit(solution)/shard_map/all_to_all | solution.py:355
  80.3 4.8 copy-start.1
  80.3 6.6 %copy-start.6 = (s32[16]{0:T(128)S(1)}, s32[16]{0:T(128)}, u32[]{:S(2)}) copy-start(s32[16]{0:T(128)} %param.25) | copy-start | bytes 196
  80.3 64.9 %all-to-all-start = ((bf16[3,8,128,512]{3,2,0,1:T(8,128)(2,1)}), bf16[3,8,128,512]{3,2,0,1:T(8,128)(2,1)}, u32[]{:S(2)}, u32[]{:S(2)}) async-start(bf16[3,8,128,512]{3,2,0,1:T(8,128)(2,1)} %select_bitcast_fusion), calls=%async_computation | async-start | bytes 6291456 | tf_op jit(solution)/shard_map/all_to_all | solution.py:354
  88.4 7.2 %copy-start = (bf16[2,2,4096,512]{3,2,1,0:T(8,128)(2,1)S(1)}, bf16[2,2,4096,512]{3,2,1,0:T(8,128)(2,1)}, u32[]{:S(2)}) copy-start(bf16[2,2,4096,512]{3,2,1,0:T(8,128)(2,1)} %cache_ref.3) | copy-start | bytes 50331652
  145.2 42.2 %all-to-all-start.3 = ((bf16[8,2,512]{2,1,0:T(2,128)(2,1)}), bf16[8,2,512]{2,1,0:T(2,128)(2,1)S(1)}, u32[]{:S(2)}, u32[]{:S(2)}) async-start(bf16[8,2,512]{2,1,0:T(2,128)(2,1)} %reshape.215), calls=%async_computation.3 | async-start | bytes 32768 | tf_op jit(solution)/shard_map/all_to_all | solution.py:376
  148.7 3.1 copy-start.2
  187.4 40.2 %all-to-all-start.1 = ((bf16[8,128,512]{2,1,0:T(8,128)(2,1)}), bf16[8,128,512]{2,1,0:T(8,128)(2,1)S(1)}, u32[]{:S(2)}, u32[]{:S(2)}) async-start(bf16[8,128,512]{2,1,0:T(8,128)(2,1)} %bitcast.9), calls=%async_computation.1 | async-start | bytes 2097152 | tf_op jit(solution)/shard_map/all_to_all | solution.py:375
  229.5 28.8 %all-to-all-start.4 = ((bf16[4,272,512]{2,1,0:T(8,128)(2,1)}), bf16[4,272,512]{2,1,0:T(8,128)(2,1)S(1)}, u32[]{:S(2)}, u32[]{:S(2)}) async-start(bf16[4,272,512]{2,1,0:T(8,128)(2,1)} %pad_maximum_fusion.4), calls=%async_computation.4 | async-start | bytes 2228224 | tf_op jit(solution)/shard_map/all_to_all | solution.py:53
  234.1 116.1 %all-gather.17.cloned.1.call-start = ((), (), s32[]{:S(2)}) async-start(), calls=%async_computation.12 | async-start | bytes 2621440 | tf_op jit(solution)/shard_map/all_gather | solution.py:57
  258.4 6.5 %copy-start.5 = (f32[2048]{0:T(1024)S(1)}, f32[2048]{0:T(1024)}, u32[]{:S(2)}) copy-start(f32[2048]{0:T(1024)} %param.17) | copy-start | bytes 24580
  304.0 93.0 %all-gather.19.cloned.1.call-start = ((), (), s32[]{:S(2)}) async-start(), calls=%async_computation.14 | async-start | bytes 2621440 | tf_op jit(solution)/shard_map/all_gather | solution.py:57
  350.3 91.5 %reduce-scatter.3.cloned.1.call-start = ((), (), s32[]{:S(2)}) async-start(), calls=%async_computation.13 | async-start | bytes 2621440 | tf_op jit(solution)/shard_map/reduce_scatter | solution.py:61
  372.8 119.5 %reduce-scatter.5.cloned.1.call-start = ((), (), s32[]{:S(2)}) async-start(), calls=%async_computation.15 | async-start | bytes 2949120 | tf_op jit(solution)/shard_map/reduce_scatter | solution.py:61
  441.9 97.5 %all-gather.21.cloned.1.call-start = ((), (), s32[]{:S(2)}) async-start(), calls=%async_computation.16 | async-start | bytes 2621440 | tf_op jit(solution)/shard_map/all_gather | solution.py:57
  492.3 98.4 %all-gather.23.cloned.1.call-start = ((), (), s32[]{:S(2)}) async-start(), calls=%async_computation.17 | async-start | bytes 2949120 | tf_op jit(solution)/shard_map/all_gather | solution.py:57
  539.4 54.5 %copy-start.3 = (bf16[512,2048]{1,0:T(8,128)(2,1)S(1)}, bf16[512,2048]{1,0:T(8,128)(2,1)}, u32[]{:S(2)}) copy-start(bf16[512,2048]{1,0:T(8,128)(2,1)} %all-gather.21.cloned.1.call-done) | copy-start | bytes 6291460
Sparse Core Ops, SparseCore 0:
  9.9 49.3 all-gather.8
  61.1 78.5 all-gather.10
  141.6 62.4 all-gather.14
  205.9 96.9 all-gather.12
  304.3 45.9 all-gather.16
  352.3 44.6 all-gather.18
  399.2 42.5 reduce-scatter.2
  444.8 47.3 reduce-scatter.4
  493.9 45.4 all-gather.20
  541.4 49.1 all-gather.22
